TPU v7x, 128 devices: a whole 4x4x4 slice. The times are simulated.
128 devices in a mesh: dp: 16 (over z, x_lo, core), space: 8 (over x_hi, y).
Axes of the slice: x: 4 (x_hi: 2, x_lo: 2; x = x_hi * 2 + x_lo), y: 4, z: 4, core: 2. Of those that a mesh axis runs over, the one named last changes fastest.
Arguments:
- features: bfloat16 [16, 128, 64, 1024], P('dp', 'space'), may hold values from -6 to 6
- target: bfloat16 [16, 128, 64, 1024], P('dp', 'space'), may hold values from -6 to 6
- anchors: int32 [16, 2], P('dp'), may hold values from 0 to 64512
- w_first: bfloat16 [3, 3, 64, 64], replicated, may hold values from -0.25 to 0.25
- b_first: float32 [64], replicated, may hold values from -3 to 3
- w_second: bfloat16 [3, 3, 64, 64], replicated, may hold values from -0.25 to 0.25
- b_second: float32 [64], replicated, may hold values from -3 to 3
Outputs:
- back_input: bfloat16 [16, 128, 64, 1024], P('dp', 'space')
- grad_w1: float32 [3, 3, 64, 64], replicated
- grad_b1: float32 [64], replicated
- grad_w2: float32 [3, 3, 64, 64], replicated
- grad_b2: float32 [64], replicated
All inputs are finite; a program needn't handle non-finite values.
Results may differ from a plain program's by a relative error of at most 0.0075.
Values may be sent and summed in bfloat16 or wider, within the bound.
No kernel may reach another device: no remote copies, remote signals or barrier semaphores. Data moves between devices by JAX's collectives and lax.ppermute only.
A program may use at most 128 MiB of HBM per device.

v0:
```python
import math

import jax
import jax.numpy as jnp
from jax import lax
from jax.sharding import PartitionSpec as P


def extended(value, sides, width):
    for axis, dim in sides:
        size, length = (lax.axis_size(axis), value.shape[dim])
        up = [(i, (i + 1) % size) for i in range(size - 1)]
        down = [(j, i) for i, j in up]
        last = lax.slice_in_dim(value, length - width, length, axis=dim)
        first = lax.slice_in_dim(value, 0, width, axis=dim)
        before = lax.ppermute(last, axis, up)
        after = lax.ppermute(first, axis, down)
        value = jnp.concatenate([before, value, after], axis=dim)
    return value


def shift_cols(tensor, offset):
    if offset == 0:
        return tensor
    filler = jnp.zeros(tensor.shape[:-1] + (1,), tensor.dtype)
    if offset > 0:
        return jnp.concatenate([tensor[..., 1:], filler], axis=-1)
    return jnp.concatenate([filler, tensor[..., :-1]], axis=-1)


def unfold(padded):
    inner = padded.shape[1] - 2
    pieces = [
        shift_cols(padded[:, row_off : row_off + inner], col_off - 1)
        for row_off in range(3)
        for col_off in range(3)
    ]
    return jnp.concatenate(pieces, axis=2)


def unfold_back(padded):
    inner = padded.shape[1] - 2
    pieces = [
        shift_cols(padded[:, 2 - row_off : 2 - row_off + inner], 1 - col_off)
        for row_off in range(3)
        for col_off in range(3)
    ]
    return jnp.concatenate(pieces, axis=2)


def forward_matrix(kernel):
    return jnp.transpose(kernel, (2, 0, 1, 3)).reshape(kernel.shape[2], -1)


def backward_matrix(kernel):
    return jnp.transpose(kernel, (3, 0, 1, 2)).reshape(kernel.shape[3], -1)


def fold_kernel(matrix):
    channels = matrix.shape[0]
    return jnp.transpose(matrix.reshape(channels, 3, 3, -1), (1, 2, 0, 3))


def coords(anchor_rows, row_ids, columns, channels):
    chan_ids = jnp.arange(channels, dtype=jnp.int32)
    periods = 4 * jnp.left_shift(jnp.ones_like(chan_ids), chan_ids % 8)
    scaled = 2.0 * math.pi / periods.astype(jnp.float32)
    row_pos = anchor_rows[:, 0][:, None, None] + row_ids[None, :, None]
    row_wave = jnp.sin(
        (row_pos % periods[None, None, :]).astype(jnp.float32) * scaled[None, None, :]
    )
    col_ids = jnp.arange(columns, dtype=jnp.int32)
    col_pos = anchor_rows[:, 1][:, None, None] + col_ids[None, None, :]
    col_wave = jnp.sin(
        (col_pos % periods[None, :, None]).astype(jnp.float32) * scaled[None, :, None]
    )
    use_rows = (chan_ids < channels // 2)[None, None, :, None]
    return jnp.where(use_rows, row_wave[..., None], col_wave[:, None])


def gelu_grad(pre_act, upstream):
    return jax.vjp(lambda inputs: jax.nn.gelu(inputs, approximate=True), pre_act)[1](upstream)[0]


def mixing(form, left, right):
    return jnp.einsum(form, left, right, preferred_element_type=jnp.float32)


def combine(pairs):
    flat_grads = jnp.concatenate([piece.reshape(-1) for pair in pairs for piece in pair])
    total = lax.psum(flat_grads, ("dp", "space"))
    results = []
    start = 0
    for pair in pairs:
        for piece in pair:
            count = piece.size
            results.append(total[start : start + count].reshape(piece.shape))
            start = start + count
    return results


def shards(features, target, anchors, w_first, b_first, w_second, b_second):
    strip_rows = features.shape[1]
    columns = features.shape[3]
    channels = features.shape[2]
    dev_index = lax.axis_index("space")
    crop_rows = strip_rows * lax.axis_size("space")
    factor = 1.0 / math.sqrt(features.shape[0] * lax.axis_size("dp") * crop_rows * columns)
    row_ids = dev_index * strip_rows + jnp.arange(strip_rows, dtype=jnp.int32)
    geo = coords(anchors, row_ids, columns, channels)
    first = (features.astype(jnp.float32) + geo).astype(jnp.bfloat16)
    bias_one = b_first[None, None, :, None]
    first_pad = extended(first, (("space", 1),), 1)
    pre_act = mixing("dk,brkw->brdw", forward_matrix(w_first), unfold(first_pad)) + bias_one
    hidden = jax.nn.gelu(pre_act, approximate=True).astype(jnp.bfloat16)
    hidden_pad = extended(hidden, (("space", 1),), 1)
    output = (
        mixing("dk,brkw->brdw", forward_matrix(w_second), unfold(hidden_pad))
        + b_second[None, None, :, None]
    )
    misfit = (output - target.astype(jnp.float32)).astype(jnp.bfloat16)
    grad_w2 = fold_kernel(mixing("brdw,brkw->dk", misfit, unfold(hidden_pad))) * factor
    grad_b2 = jnp.sum(misfit.astype(jnp.float32), axis=(0, 1, 3)) * factor
    misfit_pad = extended(misfit, (("space", 1),), 1)
    back_hidden = mixing("ck,brkw->brcw", backward_matrix(w_second), unfold_back(misfit_pad))
    slope = gelu_grad(pre_act, back_hidden).astype(jnp.bfloat16)
    grad_w1 = fold_kernel(mixing("brdw,brkw->dk", slope, unfold(first_pad))) * factor
    grad_b1 = jnp.sum(slope.astype(jnp.float32), axis=(0, 1, 3)) * factor
    slope_pad = extended(slope, (("space", 1),), 1)
    back_input = mixing("ck,brkw->brcw", backward_matrix(w_first), unfold_back(slope_pad)).astype(
        jnp.bfloat16
    )
    grad_w2, grad_b2, grad_w1, grad_b1 = combine([(grad_w2, grad_b2), (grad_w1, grad_b1)])
    return (back_input, grad_w1, grad_b1, grad_w2, grad_b2)


def solution(mesh):
    in_specs = (
        P("dp", "space", None, None),
        P("dp", "space", None, None),
        P("dp", None),
        P(),
        P(),
        P(),
        P(),
    )
    out_specs = (P("dp", "space", None, None), P(), P(), P(), P())
    return jax.shard_map(shards, mesh=mesh, in_specs=in_specs, out_specs=out_specs, check_vma=False)
```

profile of v0, /device:TPU:1, one launch (start us, length us, event | category | flops | bytes accessed | tf_op | source)
XLA Modules:
  0.0 301.8 jit_solution(5083959459954517360)
XLA Ops:
  7.3 1.3 fusion.122
  10.2 3.5 %fusion.106 = f32[64,1024]{1,0:T(8,128)S(1)} fusion(f32[64]{0:T(128)S(1)} %convert_divide_fusion, s32[64]{0:T(128)S(1)} %compare_select_fusion, s32[1024]{0:T(1024)S(1)} %iota_add_fusion, pred[64]{0:T(512)(128)(4,1)S(1)} %broadcast_compare_fusion), kind=kLoop, calls=%fused_computation.138 | loop fusion | flops 589824 | bytes 266816 | tf_op jit(solution)/shard_map/sin | solution.py:74
  13.6 2.1 add_convert_fusion
  15.8 1.3 collective-permute-start.1
  17.1 4.8 %collective-permute-start = (bf16[1,1,64,1024]{3,2,1,0:T(8,128)(2,1)S(1)}, bf16[1,1,64,1024]{3,2,1,0:T(8,128)(2,1)S(1)}, u32[]{:S(2)}, u32[]{:S(2)}) collective-permute-start(bf16[1,1,64,1024]{3,2,1,0:T(8,128)(2,1)S(1)} %get-tuple-element.28), channel_id=1, source_target_pairs={{0,1},{1,2},{2,3},{3,4},{4,5},{5,6},{6,7},{8,9},{9,10},{10,11},{11... | collective-permute-start | bytes 393224 | tf_op jit(solution)/shard_map/ppermute | solution.py:16
  27.0 1.2 pad_dynamic-update-slice_fusion.14
  29.1 1.2 pad_dynamic-update-slice_fusion.12
  31.6 8.4 %fusion.35 = (bf16[1,16,64,1024]{3,2,1,0:T(8,128)(2,1)S(1)}, f32[16,1024,64]{1,2,0:T(8,128)}) fusion(f32[64]{0:T(128)S(1)} %copy-done.6, bf16[64,576,1]{0,1,2:T(8,128)(2,1)S(1)} %bitcast.173, bf16[1,16,576,1024]{3,2,1,0:T(8,128)(2,1)S(1)} %fusion.65), kind=kOutput, calls=%fused_computation.44 | convolution fusion | flops 1218445312 | bytes 25239808 | tf_op jit(solution)/shard_map/dk,brkw->brdw/dot_general | solution.py:86
  40.0 1.3 collective-permute-start.3
  41.3 4.6 %collective-permute-start.2 = (bf16[1,1,64,1024]{3,2,1,0:T(8,128)(2,1)S(1)}, bf16[1,1,64,1024]{3,2,1,0:T(8,128)(2,1)S(1)}, u32[]{:S(2)}, u32[]{:S(2)}) collective-permute-start(bf16[1,1,64,1024]{3,2,1,0:T(8,128)(2,1)S(1)} %get-tuple-element.22), channel_id=1, source_target_pairs={{0,1},{1,2},{2,3},{3,4},{4,5},{5,6},{6,7},{8,9},{9,10},{10,11},{11... | collective-permute-start | bytes 393224 | tf_op jit(solution)/shard_map/ppermute | solution.py:16
  46.1 1.5 collective-permute-done.2
  55.1 8.4 %convert_reduce_fusion.1 = (f32[64]{0:T(128)S(1)}, bf16[1,16,64,1024]{3,2,1,0:T(8,128)(2,1)S(1)}) fusion(bf16[1,16,64,1024]{3,2,1,0:T(8,128)(2,1)} %param.8, f32[64]{0:T(128)S(1)} %copy-done.5, bf16[64,576,1]{0,1,2:T(8,128)(2,1)S(1)} %bitcast.167, bf16[1,16,576,1024]{3,2,1,0:T(8,128)(2,1)S(1)} %fusion.69), kind=kOutput, calls=%fused_computation.47 | convolution fusion | flops 1214251008 | bytes 23142912 | tf_op jit(solution)/shard_map/dk,brkw->brdw/dot_general | solution.py:86
  63.5 12.3 %fusion.92 = f32[3,3,64,64]{3,2,1,0:T(8,128)S(1)} fusion(bf16[3,3,64,16,1024]{4,2,1,0,3:T(8,128)(2,1)} %bitcast.166, bf16[1,16,64,1024]{3,2,1,0:T(8,128)(2,1)S(1)} %get-tuple-element.38), kind=kOutput, calls=%fused_computation.128 | convolution fusion | flops 1207996416 | bytes 21118976 | tf_op jit(solution)/shard_map/brdw,brkw->dk/dot_general | solution.py:86
  76.0 4.1 %collective-permute-start.5 = (bf16[1,1,64,1024]{3,2,1,0:T(8,128)(2,1)S(1)}, bf16[1,1,64,1024]{3,2,1,0:T(8,128)(2,1)S(1)}, u32[]{:S(2)}, u32[]{:S(2)}) collective-permute-start(bf16[1,1,64,1024]{3,2,1,0:T(8,128)(2,1)S(1)} %get-tuple-element.15), channel_id=1, source_target_pairs={{0,1},{1,2},{2,3},{3,4},{4,5},{5,6},{6,7},{8,9},{9,10},{10,11},{11... | collective-permute-start | bytes 393224 | tf_op jit(solution)/shard_map/ppermute | solution.py:16
  80.0 1.7 collective-permute-start.4
  82.0 5.7 %collective-permute-done.4 = bf16[1,1,64,1024]{3,2,1,0:T(8,128)(2,1)S(1)} collective-permute-done((bf16[1,1,64,1024]{3,2,1,0:T(8,128)(2,1)S(1)}, bf16[1,1,64,1024]{3,2,1,0:T(8,128)(2,1)S(1)}, u32[]{:S(2)}, u32[]{:S(2)}) %collective-permute-start.4) | collective-permute-done | bytes 131104 | tf_op jit(solution)/shard_map/ppermute | solution.py:17
  87.6 2.4 fusion.46
  90.6 1.3 fusion.71
  92.5 1.2 pad_dynamic-update-slice_fusion.5
  94.2 1.3 fusion.73
  95.5 10.1 %convert_reduce_fusion = (f32[64]{0:T(128)S(1)}, bf16[1,16,64,1024]{3,2,1,0:T(8,128)(2,1)S(1)}) fusion(f32[64]{0:T(128)S(1)} %copy-done.6, f32[16,1024,64]{1,2,0:T(8,128)} %get-tuple-element.36, bf16[64,576,1]{0,1,2:T(8,128)(2,1)S(1)} %bitcast.172, bf16[1,16,576,1024]{3,2,1,0:T(8,128)(2,1)S(1)} %fusion.73), kind=kOutput, calls=%fused_computation.46 | convolution fusion | flops 1232076800 | bytes 25240064 | tf_op jit(solution)/shard_map/ck,brkw->brcw/dot_general | solution.py:86
  105.6 12.5 %fusion.101 = f32[3,3,64,64]{3,2,1,0:T(8,128)S(1)} fusion(bf16[3,3,64,16,1024]{4,2,1,0,3:T(8,128)(2,1)} %bitcast.170, bf16[1,16,64,1024]{3,2,1,0:T(8,128)(2,1)S(1)} %get-tuple-element.40), kind=kOutput, calls=%fused_computation.131 | convolution fusion | flops 1207996416 | bytes 21118976 | tf_op jit(solution)/shard_map/brdw,brkw->dk/dot_general | solution.py:86
  118.3 7.4 %collective-permute-start.7 = (bf16[1,1,64,1024]{3,2,1,0:T(8,128)(2,1)S(1)}, bf16[1,1,64,1024]{3,2,1,0:T(8,128)(2,1)S(1)}, u32[]{:S(2)}, u32[]{:S(2)}) collective-permute-start(bf16[1,1,64,1024]{3,2,1,0:T(8,128)(2,1)S(1)} %get-tuple-element.9), channel_id=1, source_target_pairs={{0,1},{1,2},{2,3},{3,4},{4,5},{5,6},{6,7},{8,9},{9,10},{10,11},{11... | collective-permute-start | bytes 393224 | tf_op jit(solution)/shard_map/ppermute | solution.py:16
  125.7 1.3 collective-permute-start.6
  127.0 4.3 %concatenate.165 = f32[73856]{0:T(1024)} concatenate(f32[36864]{0:T(1024)S(1)} %reshape.374, f32[64]{0:T(128)S(1)} %broadcast_multiply_fusion.1, f32[36864]{0:T(1024)S(1)} %reshape.376, f32[64]{0:T(128)S(1)} %broadcast_multiply_fusion), dimensions={0} | concatenate | bytes 590848 | tf_op jit(solution)/shard_map/concatenate | solution.py:90
  131.3 4.1 %collective-permute-done.6 = bf16[1,1,64,1024]{3,2,1,0:T(8,128)(2,1)S(1)} collective-permute-done((bf16[1,1,64,1024]{3,2,1,0:T(8,128)(2,1)S(1)}, bf16[1,1,64,1024]{3,2,1,0:T(8,128)(2,1)S(1)}, u32[]{:S(2)}, u32[]{:S(2)}) %collective-permute-start.6) | collective-permute-done | bytes 131104 | tf_op jit(solution)/shard_map/ppermute | solution.py:17
  135.4 2.4 fusion.40
  138.4 1.3 fusion.75
  141.9 1.3 fusion.77
  143.2 6.7 %convert_bitcast_fusion = bf16[1,16,64,1024]{3,2,1,0:T(8,128)(2,1)} fusion(bf16[64,576,1]{0,1,2:T(8,128)(2,1)S(1)} %bitcast.169, bf16[1,16,576,1024]{3,2,1,0:T(8,128)(2,1)S(1)} %fusion.77), kind=kOutput, calls=%fused_computation.109 | convolution fusion | flops 1209008128 | bytes 21045248 | tf_op jit(solution)/shard_map/ck,brkw->brcw/dot_general | solution.py:86
  150.0 140.8 %all-reduce.26.cloned.1.call-done = f32[73856]{0:T(1024)} async-done(((f32[73856]{0:T(1024)}), f32[73856]{0:T(1024)}) %all-reduce.26.cloned.1.call-update) | async-done | bytes 295440 | tf_op jit(solution)/shard_map/psum | solution.py:91
  293.5 1.3 fusion.120
  (72 shorter events, 24.2 us)
Async XLA Ops:
  7.2 14.8 %copy-start.2 = (bf16[3,3,64,64]{3,2,1,0:T(8,128)(2,1)S(1)}, bf16[3,3,64,64]{3,2,1,0:T(8,128)(2,1)}, u32[]{:S(2)}) copy-start(bf16[3,3,64,64]{3,2,1,0:T(8,128)(2,1)} %param.10) | copy-start | bytes 221188
  7.2 283.6 %all-reduce.26.cloned.1.call-start = ((), (), s32[]{:S(2)}) async-start(), calls=%async_computation | async-start | bytes 598016 | tf_op jit(solution)/shard_map/psum | solution.py:91
  15.8 6.9 %collective-permute-start.1 = (bf16[1,1,64,1024]{3,2,1,0:T(8,128)(2,1)S(1)}, bf16[1,1,64,1024]{3,2,1,0:T(8,128)(2,1)S(1)}, u32[]{:S(2)}, u32[]{:S(2)}) collective-permute-start(bf16[1,1,64,1024]{3,2,1,0:T(8,128)(2,1)S(1)} %get-tuple-element.27), channel_id=1, source_target_pairs={{1,0},{2,1},{3,2},{4,3},{5,4},{6,5},{7,6},{9,8},{10,9},{11,10},{12... | collective-permute-start | bytes 393224 | tf_op jit(solution)/shard_map/ppermute | solution.py:17
  17.1 6.6 %collective-permute-start = (bf16[1,1,64,1024]{3,2,1,0:T(8,128)(2,1)S(1)}, bf16[1,1,64,1024]{3,2,1,0:T(8,128)(2,1)S(1)}, u32[]{:S(2)}, u32[]{:S(2)}) collective-permute-start(bf16[1,1,64,1024]{3,2,1,0:T(8,128)(2,1)S(1)} %get-tuple-element.28), channel_id=1, source_target_pairs={{0,1},{1,2},{2,3},{3,4},{4,5},{5,6},{6,7},{8,9},{9,10},{10,11},{11... | collective-permute-start | bytes 393224 | tf_op jit(solution)/shard_map/ppermute | solution.py:16
  25.9 2.3 copy-start.1
  30.2 1.4 copy-start.6
  31.6 8.4 %copy-start.3 = (bf16[1,16,576,1024]{3,2,1,0:T(8,128)(2,1)}, bf16[1,16,576,1024]{3,2,1,0:T(8,128)(2,1)S(1)}, u32[]{:S(2)}) copy-start(bf16[1,16,576,1024]{3,2,1,0:T(8,128)(2,1)S(1)} %fusion.65) | copy-start | bytes 56623108
  31.6 14.3 %copy-start.4 = (bf16[3,3,64,64]{3,2,1,0:T(8,128)(2,1)S(1)}, bf16[3,3,64,64]{3,2,1,0:T(8,128)(2,1)}, u32[]{:S(2)}) copy-start(bf16[3,3,64,64]{3,2,1,0:T(8,128)(2,1)} %param.12) | copy-start | bytes 221188
  40.0 6.1 %collective-permute-start.3 = (bf16[1,1,64,1024]{3,2,1,0:T(8,128)(2,1)S(1)}, bf16[1,1,64,1024]{3,2,1,0:T(8,128)(2,1)S(1)}, u32[]{:S(2)}, u32[]{:S(2)}) collective-permute-start(bf16[1,1,64,1024]{3,2,1,0:T(8,128)(2,1)S(1)} %get-tuple-element.21), channel_id=1, source_target_pairs={{1,0},{2,1},{3,2},{4,3},{5,4},{6,5},{7,6},{9,8},{10,9},{11,10},{12... | collective-permute-start | bytes 393224 | tf_op jit(solution)/shard_map/ppermute | solution.py:17
  41.3 6.3 %collective-permute-start.2 = (bf16[1,1,64,1024]{3,2,1,0:T(8,128)(2,1)S(1)}, bf16[1,1,64,1024]{3,2,1,0:T(8,128)(2,1)S(1)}, u32[]{:S(2)}, u32[]{:S(2)}) collective-permute-start(bf16[1,1,64,1024]{3,2,1,0:T(8,128)(2,1)S(1)} %get-tuple-element.22), channel_id=1, source_target_pairs={{0,1},{1,2},{2,3},{3,4},{4,5},{5,6},{6,7},{8,9},{9,10},{10,11},{11... | collective-permute-start | bytes 393224 | tf_op jit(solution)/shard_map/ppermute | solution.py:16
  53.8 1.3 copy-start.5
  55.1 8.4 %copy-start = (bf16[1,16,576,1024]{3,2,1,0:T(8,128)(2,1)}, bf16[1,16,576,1024]{3,2,1,0:T(8,128)(2,1)S(1)}, u32[]{:S(2)}) copy-start(bf16[1,16,576,1024]{3,2,1,0:T(8,128)(2,1)S(1)} %fusion.69) | copy-start | bytes 56623108
  76.0 6.0 %collective-permute-start.5 = (bf16[1,1,64,1024]{3,2,1,0:T(8,128)(2,1)S(1)}, bf16[1,1,64,1024]{3,2,1,0:T(8,128)(2,1)S(1)}, u32[]{:S(2)}, u32[]{:S(2)}) collective-permute-start(bf16[1,1,64,1024]{3,2,1,0:T(8,128)(2,1)S(1)} %get-tuple-element.15), channel_id=1, source_target_pairs={{0,1},{1,2},{2,3},{3,4},{4,5},{5,6},{6,7},{8,9},{9,10},{10,11},{11... | collective-permute-start | bytes 393224 | tf_op jit(solution)/shard_map/ppermute | solution.py:16
  80.0 7.6 %collective-permute-start.4 = (bf16[1,1,64,1024]{3,2,1,0:T(8,128)(2,1)S(1)}, bf16[1,1,64,1024]{3,2,1,0:T(8,128)(2,1)S(1)}, u32[]{:S(2)}, u32[]{:S(2)}) collective-permute-start(bf16[1,1,64,1024]{3,2,1,0:T(8,128)(2,1)S(1)} %get-tuple-element.16), channel_id=1, source_target_pairs={{1,0},{2,1},{3,2},{4,3},{5,4},{6,5},{7,6},{9,8},{10,9},{11,10},{12... | collective-permute-start | bytes 393224 | tf_op jit(solution)/shard_map/ppermute | solution.py:17
  118.3 13.1 %collective-permute-start.7 = (bf16[1,1,64,1024]{3,2,1,0:T(8,128)(2,1)S(1)}, bf16[1,1,64,1024]{3,2,1,0:T(8,128)(2,1)S(1)}, u32[]{:S(2)}, u32[]{:S(2)}) collective-permute-start(bf16[1,1,64,1024]{3,2,1,0:T(8,128)(2,1)S(1)} %get-tuple-element.9), channel_id=1, source_target_pairs={{0,1},{1,2},{2,3},{3,4},{4,5},{5,6},{6,7},{8,9},{9,10},{10,11},{11... | collective-permute-start | bytes 393224 | tf_op jit(solution)/shard_map/ppermute | solution.py:16
  125.7 9.7 %collective-permute-start.6 = (bf16[1,1,64,1024]{3,2,1,0:T(8,128)(2,1)S(1)}, bf16[1,1,64,1024]{3,2,1,0:T(8,128)(2,1)S(1)}, u32[]{:S(2)}, u32[]{:S(2)}) collective-permute-start(bf16[1,1,64,1024]{3,2,1,0:T(8,128)(2,1)S(1)} %get-tuple-element.10), channel_id=1, source_target_pairs={{1,0},{2,1},{3,2},{4,3},{5,4},{6,5},{7,6},{9,8},{10,9},{11,10},{12... | collective-permute-start | bytes 393224 | tf_op jit(solution)/shard_map/ppermute | solution.py:17
Sparse Core Ops, SparseCore 0:
  131.4 159.3 all-reduce.25
where the time goes:
time: 306 us; the launch traced here: 302 us
  waiting for transfers between devices  154 us (50%)
  matrix products  58.4 us (19%)
  starting transfers between devices  26.5 us (9%)
  other arithmetic  25.8 us (8%)
  local copies, waits for them, and re-layouts  22.4 us (7%)
  between operations  14.9 us (5%)
    psum x1, waiting for transfers between devices, combine(): total = lax.psum(flat_grads, ('dp', 'space'))  141 us
    dot_general x6, matrix products, mixing(): return jnp.einsum(form, left, right, preferred_element_type=jnp.float32)  58.4 us
    ppermute x4, starting transfers between devices, extended(): before = lax.ppermute(last, axis, up)  20.9 us
    unnamed x33, local copies, waits for them, and re-layouts  12.2 us
    ppermute x4, waiting for transfers between devices, extended(): after = lax.ppermute(first, axis, down)  10.4 us
    unnamed x13, other arithmetic  7.09 us
    concatenate x4, other arithmetic, extended(): value = jnp.concatenate([before, value, after], axis=dim)  6.78 us
  transfers between devices with their start and end apart: 9, of which 7 were waited for; matrix products, arithmetic and copies ran while one was open for 6% of the time, Pallas kernels for 0%

commit v1 on v0

v1 whole, which is shorter than its diff:
```python
import functools
import math

import jax
import jax.numpy as jnp
from jax import lax
from jax.experimental import pallas as pl
from jax.experimental.pallas import tpu as pltpu
from jax.sharding import PartitionSpec as P

BF = jnp.bfloat16
F32 = jnp.float32
AXES = ("dp", "space")
FEAT_HALO = 4
GOAL_HALO = 2
GELU_SCALE = math.sqrt(2.0 / math.pi)
GELU_CUBE = 0.044715


def to_right(value):
    lane = lax.broadcasted_iota(jnp.int32, value.shape, 1)
    return jnp.where(lane == 0, jnp.zeros_like(value), pltpu.roll(value, 1, 1))


def to_left(value):
    last = value.shape[1] - 1
    lane = lax.broadcasted_iota(jnp.int32, value.shape, 1)
    return jnp.where(lane == last, jnp.zeros_like(value), pltpu.roll(value, last, 1))


def keep(flag, value):
    return jnp.where(flag > 0, value, jnp.zeros_like(value))


def masked(value, low, high):
    if low is None and high is None:
        return value
    half = value.shape[0] // 2
    first, second = value[:half], value[half:]
    if low is not None:
        first = keep(low, first)
    if high is not None:
        second = keep(high, second)
    return jnp.concatenate([first, second], axis=0)


def lane_sum(value):
    half = value.shape[0] // 2
    both = value[:half] + value[half:]
    total = both[:, :128]
    for start in range(128, both.shape[1], 128):
        total = total + both[:, start : start + 128]
    return total


def step_kernel(
    rows,
    ch,
    factor,
    flags_ref,
    feat_ref,
    goal_ref,
    top_ref,
    bot_ref,
    row_wave_ref,
    col_wave_ref,
    fwd1_ref,
    fwd2_ref,
    bwd1_ref,
    bwd2_ref,
    bias1_ref,
    bias2_ref,
    back_ref,
    grads_ref,
    first,
    hidden,
    deriv,
    misfit,
    slope,
    acc1,
    acc2,
    sum1,
    sum2,
):
    pair = 2 * ch
    quad = 4 * ch
    cols = feat_ref.shape[-1]
    above, below = flags_ref[0], flags_ref[1]

    def put_first(index, value, flag):
        wave = jnp.concatenate(
            [
                jnp.tile(row_wave_ref[index], (1, cols // 128)),
                col_wave_ref[...],
            ],
            axis=0,
        )
        result = value.astype(F32) + wave
        if flag is not None:
            result = keep(flag, result)
        first[pl.ds(pl.multiple_of(index * ch, ch), ch)] = result.astype(BF)

    for row in range(FEAT_HALO):
        put_first(row, top_ref[row], above)
        put_first(rows + FEAT_HALO + row, bot_ref[row], below)

    def put_inner(row, carry):
        put_first(row + FEAT_HALO, feat_ref[row], None)
        return carry

    lax.fori_loop(0, rows, put_inner, 0, unroll=2)

    bias1 = jnp.broadcast_to(bias1_ref[...], (pair, cols))
    bias2 = jnp.broadcast_to(bias2_ref[...], (pair, cols))

    def spread(kernel_ref, source, at):
        parts = jnp.dot(
            kernel_ref[...],
            source[pl.ds(pl.multiple_of(at * ch, ch), quad)],
            preferred_element_type=F32,
        )
        return parts[pair : 2 * pair] + to_right(parts[:pair]) + to_left(parts[2 * pair :])

    def forward_one(p, low, high, wants_deriv):
        pre = spread(fwd1_ref, first, 2 * p) + bias1_ref[...]
        square = pre * pre
        bent = jnp.tanh(pre * (GELU_SCALE + (GELU_SCALE * GELU_CUBE) * square))
        cdf = 0.5 + 0.5 * bent
        hid = masked(pre * cdf, low, high)
        hidden[pl.ds(pl.multiple_of(p * pair, pair), pair)] = hid.astype(BF)
        if wants_deriv:
            inner = GELU_SCALE + (3.0 * GELU_SCALE * GELU_CUBE) * square
            grad = cdf + (0.5 * pre) * ((1.0 - bent * bent) * inner)
            deriv[pl.ds(pl.multiple_of((p - 1) * pair, pair), pair)] = grad

    def put_three(target, at, value):
        spot = pl.ds(pl.multiple_of(at * ch, ch), pair)
        target[0, spot] = to_left(value)
        target[1, spot] = value
        target[2, spot] = to_right(value)

    def forward_two(p, goal, flag):
        out = spread(fwd2_ref, hidden, 2 * p) + bias2_ref[...]
        error = out - goal.astype(F32)
        if flag is not None:
            error = keep(flag, error)
        error = error.astype(BF)
        put_three(misfit, 2 * p, error)
        if flag is None:
            sum2[...] += lane_sum(error.astype(F32))

    def back(kernel_ref, source, at):
        spot = pl.ds(pl.multiple_of(at * ch, ch), quad)
        stack = jnp.concatenate([source[0, spot], source[1, spot], source[2, spot]], axis=0)
        return jnp.dot(kernel_ref[...], stack, preferred_element_type=F32)

    def backward_two(p, low, high):
        up = back(bwd2_ref, misfit, 2 * p)
        value = up * deriv[pl.ds(pl.multiple_of(p * pair, pair), pair)]
        value = masked(value, low, high).astype(BF)
        put_three(slope, 2 * p, value)
        wide = value.astype(F32)
        half = wide.shape[0] // 2
        if low is not None:
            wide = jnp.concatenate([jnp.zeros_like(wide[:half]), wide[half:]], axis=0)
        if high is not None:
            wide = jnp.concatenate([wide[:half], jnp.zeros_like(wide[half:])], axis=0)
        sum1[...] += lane_sum(wide)

    def backward_one(p):
        value = back(bwd1_ref, slope, 2 * p).astype(BF)
        back_ref[2 * p] = value[:ch]
        back_ref[2 * p + 1] = value[ch:]

    def weight_grad(acc, errors, error_at, source, source_at):
        spot = pl.ds(pl.multiple_of(error_at * ch, ch), pair)
        stack = jnp.concatenate([errors[0, spot], errors[1, spot], errors[2, spot]], axis=0)
        block = source[pl.ds(pl.multiple_of(source_at * ch, ch), quad)]
        acc[...] += lax.dot_general(
            stack, block, (((1,), (1,)), ((), ())), preferred_element_type=F32
        )

    sum1[...] = jnp.zeros_like(sum1)
    sum2[...] = jnp.zeros_like(sum2)
    acc1[...] = jnp.zeros_like(acc1)
    acc2[...] = jnp.zeros_like(acc2)

    def loop(start, stop, body, unroll):
        def run(p, carry):
            body(p)
            return carry

        lax.fori_loop(start, stop, run, 0, unroll=unroll)

    pairs = rows // 2
    forward_one(0, above, above, False)
    forward_one(1, above, None, True)
    loop(2, pairs + 1, lambda p: forward_one(p, None, None, True), 7)
    forward_one(pairs + 1, None, below, True)
    forward_one(pairs + 2, below, below, False)

    def goal_rows(at):
        return jnp.concatenate([goal_ref[at], goal_ref[at + 1]], axis=0)

    forward_two(0, jnp.concatenate([top_ref[4], top_ref[5]], axis=0), above)
    forward_two(pairs + 1, jnp.concatenate([bot_ref[4], bot_ref[5]], axis=0), below)
    loop(1, pairs + 1, lambda p: forward_two(p, goal_rows(2 * p - 2), None), 4)

    loop(0, pairs, lambda p: weight_grad(acc2, misfit, 2 * p + 2, hidden, 2 * p + 2), 4)

    backward_two(0, above, None)
    backward_two(pairs, None, below)
    loop(1, pairs, lambda p: backward_two(p, None, None), 7)

    loop(0, pairs, lambda p: weight_grad(acc1, slope, 2 * p + 1, first, 2 * p + 3), 4)
    loop(0, pairs, backward_one, 4)

    def emit(base, acc, total):
        summed = jnp.sum(total[...], axis=1, keepdims=True)
        side = jnp.broadcast_to(summed, (ch, ch))
        for j in range(3):
            low = acc[2 * j * ch : (2 * j + 1) * ch]
            high = acc[(2 * j + 1) * ch : (2 * j + 2) * ch]
            block = jnp.concatenate([low[:, : 3 * ch] + high[:, ch:], side], axis=1) * factor
            for t in range(ch // 8):
                for half in range(2):
                    grads_ref[base + (j * (ch // 8) + t) * 2 + half] = block[
                        8 * t : 8 * t + 8, 128 * half : 128 * half + 128
                    ]

    emit(0, acc1, sum1)
    emit(6 * (ch // 8), acc2, sum2)
    for spare in range(12 * (ch // 8), grads_ref.shape[0]):
        grads_ref[spare] = jnp.zeros((8, 128), F32)


def split_kernel(ch, full_ref, w1_ref, b1_ref, w2_ref, b2_ref):
    for base, w_ref, b_ref in ((0, w1_ref, b1_ref), (6 * (ch // 8), w2_ref, b2_ref)):
        for j in range(3):
            left, right = [
                jnp.concatenate(
                    [full_ref[base + (j * (ch // 8) + t) * 2 + half] for t in range(ch // 8)],
                    axis=0,
                )
                for half in range(2)
            ]
            w_ref[0, j] = left[:, :ch]
            w_ref[1, j] = left[:, ch:]
            w_ref[2, j] = right[:, :ch]
            if j == 0:
                b_ref[...] = jnp.transpose(right)[ch : ch + 8]


def pair_matrix(kernel, order):
    ch = kernel.shape[-1]
    flat = jnp.transpose(kernel, order).reshape(3, ch, 3 * ch)
    low = jnp.pad(flat, ((0, 0), (0, 0), (0, ch)))
    high = jnp.pad(flat, ((0, 0), (0, 0), (ch, 0)))
    return jnp.stack([low, high], axis=1).reshape(3, 2 * ch, 4 * ch)


def forward_matrix(kernel):
    matrix = pair_matrix(kernel, (1, 2, 0, 3))
    return matrix.reshape(-1, matrix.shape[-1])


def backward_matrix(kernel):
    matrix = pair_matrix(kernel[::-1], (1, 3, 0, 2))
    return jnp.transpose(matrix, (1, 0, 2)).reshape(matrix.shape[1], -1)


def waves(anchors, row_ids, columns, channels):
    chan_ids = jnp.arange(channels, dtype=jnp.int32)
    periods = 4 * jnp.left_shift(jnp.ones_like(chan_ids), chan_ids % 8)
    scaled = 2.0 * math.pi / periods.astype(F32)
    half = channels // 2
    row_pos = anchors[0, 0] + row_ids[:, None]
    row_wave = jnp.sin(
        jnp.remainder(row_pos, periods[None, :half]).astype(F32) * scaled[None, :half]
    )
    col_pos = anchors[0, 1] + jnp.arange(columns, dtype=jnp.int32)[None, :]
    col_wave = jnp.sin(
        jnp.remainder(col_pos, periods[half:, None]).astype(F32) * scaled[half:, None]
    )
    return jnp.broadcast_to(row_wave[:, :, None], row_wave.shape + (128,)), col_wave


def shards(features, target, anchors, w_first, b_first, w_second, b_second):
    _, rows, ch, cols = features.shape
    size = lax.axis_size("space")
    devices = size * lax.axis_size("dp")
    me = lax.axis_index("space")
    factor = 1.0 / math.sqrt(features.shape[0] * devices * rows * cols)
    feats, goals = features[0], target[0]
    down = [(i, i + 1) for i in range(size - 1)]
    up = [(i + 1, i) for i in range(size - 1)]
    top = lax.ppermute(
        jnp.concatenate([feats[rows - FEAT_HALO :], goals[rows - GOAL_HALO :]]), "space", down
    )
    bottom = lax.ppermute(jnp.concatenate([feats[:FEAT_HALO], goals[:GOAL_HALO]]), "space", up)
    ids = me * rows - FEAT_HALO + jnp.arange(rows + 2 * FEAT_HALO, dtype=jnp.int32)
    row_wave, col_wave = waves(anchors, ids, cols, ch)
    flags = jnp.stack([me > 0, me < size - 1]).astype(jnp.int32)
    vmem = pl.BlockSpec(memory_space=pltpu.VMEM)
    smem = pl.BlockSpec(memory_space=pltpu.SMEM)
    pair, quad = 2 * ch, 4 * ch
    back, grads = pl.pallas_call(
        functools.partial(step_kernel, rows, ch, factor),
        out_shape=(
            jax.ShapeDtypeStruct((rows, ch, cols), BF),
            jax.ShapeDtypeStruct((devices, 8, 128), F32),
        ),
        in_specs=[smem] + [vmem] * 12,
        out_specs=(vmem, vmem),
        scratch_shapes=[
            pltpu.VMEM(((rows + 8) * ch, cols), BF),
            pltpu.VMEM(((rows + 6) * ch, cols), BF),
            pltpu.VMEM(((rows + 2) * ch, cols), F32),
            pltpu.VMEM((3, (rows + 4) * ch, cols), BF),
            pltpu.VMEM((3, (rows + 2) * ch, cols), BF),
            pltpu.VMEM((3 * pair, quad), F32),
            pltpu.VMEM((3 * pair, quad), F32),
            pltpu.VMEM((ch, 128), F32),
            pltpu.VMEM((ch, 128), F32),
        ],
        compiler_params=pltpu.CompilerParams(vmem_limit_bytes=58 << 20),
        name="step",
    )(
        flags,
        feats,
        goals,
        top,
        bottom,
        row_wave,
        col_wave,
        forward_matrix(w_first),
        forward_matrix(w_second),
        backward_matrix(w_first),
        backward_matrix(w_second),
        jnp.tile(b_first, 2)[:, None],
        jnp.tile(b_second, 2)[:, None],
    )
    parts = lax.all_to_all(grads, AXES, 0, 0, tiled=True)
    mine = jnp.sum(parts, axis=0)
    full = lax.all_to_all(
        jnp.broadcast_to(mine[None], (devices, 8, 128)), AXES, 0, 0, tiled=True
    )
    grad_w1, grad_b1, grad_w2, grad_b2 = pl.pallas_call(
        functools.partial(split_kernel, ch),
        out_shape=(
            jax.ShapeDtypeStruct((3, 3, ch, ch), F32),
            jax.ShapeDtypeStruct((8, ch), F32),
            jax.ShapeDtypeStruct((3, 3, ch, ch), F32),
            jax.ShapeDtypeStruct((8, ch), F32),
        ),
        in_specs=[vmem],
        out_specs=(vmem,) * 4,
        name="split",
    )(full)
    return (back[None], grad_w1, grad_b1[0], grad_w2, grad_b2[0])


def solution(mesh):
    in_specs = (
        P("dp", "space", None, None),
        P("dp", "space", None, None),
        P("dp", None),
        P(),
        P(),
        P(),
        P(),
    )
    out_specs = (P("dp", "space", None, None), P(), P(), P(), P())
    return jax.shard_map(shards, mesh=mesh, in_specs=in_specs, out_specs=out_specs, check_vma=False)
```

time: 306 us -> 108 us (0.35); the launches traced: 302 us -> 108 us
  waiting for transfers between devices: 154 us -> 0.01 us
  matrix products: 58.4 us -> 0 us
  blocking collectives: 0 us -> 44.6 us
  Pallas kernels: 0 us -> 28 us
  starting transfers between devices: 26.5 us -> 5.49 us
  other arithmetic: 25.8 us -> 7.04 us
  between operations: 14.9 us -> 0.84 us
    psum x1 -> x0, waiting for transfers between devices: 141 us -> none  [combine(): total = lax.psum(flat_grads, ('dp', 'space'))]
    dot_general x6 -> x0, matrix products: 58.4 us -> none  [mixing(): return jnp.einsum(form, left, right, preferred_element_type=jnp.float32)]
    all_to_all x0 -> x2, blocking collectives: none -> 44.6 us  [the longest x1 26.6 us: shards(): parts = lax.all_to_all(grads, AXES, 0, 0, tiled=True)]
    pallas_call x0 -> x2, Pallas kernels: none -> 28 us  [the longest x1 26.1 us: shards(): pl.pallas_call(functools.partial(step_kernel, rows, ch, factor), out_shap...]
    ppermute x8 -> x2, starting transfers between devices: 26.5 us -> 5.49 us  [the longest x1 4.2 us: shards(): lax.ppermute(jnp.concatenate([feats[rows - FEAT_HALO:], goals[rows - GOAL...]
    ppermute x8 -> x2, waiting for transfers between devices: 13.1 us -> 0.01 us  [the longest x1 0.01 us: shards(): lax.ppermute(jnp.concatenate([feats[rows - FEAT_HALO:], goals[rows - GOAL...]
    unnamed x33 -> x14, local copies, waits for them, and re-layouts: 12.2 us -> 0.21 us
    concatenate x8 -> x2, other arithmetic: 11.5 us -> 0.14 us  [the longest x1 0.07 us: shards(): jnp.concatenate([feats[rows - FEAT_HALO:], goals[rows - GOAL_HALO:]])]
  transfers between devices with their start and end apart: 9 -> 2, of which waited for: 7 -> 0; matrix products, arithmetic and copies ran while one was open for 6% -> 22% of each run, Pallas kernels for 0% -> 0%
where the time goes in v1:
time: 108 us
  blocking collectives  44.6 us (41%)
  Pallas kernels  28 us (26%)
  local copies, waits for them, and re-layouts  22 us (20%)
  other arithmetic  7.04 us (7%)
  starting transfers between devices  5.49 us (5%)
    all_to_all x1, blocking collectives, shards(): parts = lax.all_to_all(grads, AXES, 0, 0, tiled=True)  26.6 us
    pallas_call x1, Pallas kernels, shards(): pl.pallas_call(functools.partial(step_kernel, rows, ch, factor), out_shap...  26.1 us
    all_to_all x1, blocking collectives, shards(): lax.all_to_all(jnp.broadcast_to(mine[None], (devices, 8, 128)), AXES, 0,...  18 us
    another operation x8, local copies, waits for them, and re-layouts, pair_matrix(): return jnp.stack([low, high], axis=1).reshape(3, 2 * ch, 4 * ch)  6.56 us
    ppermute x1, starting transfers between devices, shards(): lax.ppermute(jnp.concatenate([feats[rows - FEAT_HALO:], goals[rows - GOAL...  4.2 us
    transpose x6, local copies, waits for them, and re-layouts, pair_matrix(): flat = jnp.transpose(kernel, order).reshape(3, ch, 3 * ch)  3.85 us
    sin x1, other arithmetic, waves(): jnp.sin(jnp.remainder(col_pos, periods[half:, None]).astype(F32) * scaled...  2.43 us
    transpose x2, local copies, waits for them, and re-layouts, backward_matrix(): return jnp.transpose(matrix, (1, 0, 2)).reshape(matrix.shape[1], -1)  2.17 us
  transfers between devices with their start and end apart: 2, of which 0 were waited for; matrix products, arithmetic and copies ran while one was open for 22% of the time, Pallas kernels for 0%

profile of v1, /device:TPU:1, one launch (start us, length us, event | category | flops | bytes accessed | tf_op | source)
XLA Modules:
  0.0 108.0 jit_solution(8786802908142483373)
XLA Ops:
  0.6 1.1 slice_bitcast_fusion.2
  1.7 1.3 %slice_bitcast_fusion = (bf16[4,64,1024]{2,1,0:T(8,128)(2,1)S(1)}, bf16[4,64,1024]{2,1,0:T(8,128)(2,1)S(1)}) fusion(bf16[1,16,64,1024]{3,2,1,0:T(8,128)(2,1)} %param.7), kind=kLoop, calls=%fused_computation.2 | loop fusion | bytes 2097152 | tf_op jit(solution)/shard_map/slice | solution.py:300
  3.1 4.2 %collective-permute-start = (bf16[6,64,1024]{2,1,0:T(8,128)(2,1)S(1)}, bf16[6,64,1024]{2,1,0:T(8,128)(2,1)S(1)}, u32[]{:S(2)}, u32[]{:S(2)}) collective-permute-start(bf16[6,64,1024]{2,1,0:T(8,128)(2,1)S(1)} %pad_maximum_fusion), channel_id=1, source_target_pairs={{0,1},{1,2},{2,3},{3,4},{4,5},{5,6},{6,7},{8,9},{9,10},{10,11},{11... | collective-permute-start | bytes 2359304 | tf_op jit(solution)/shard_map/ppermute | solution.py:297
  7.4 1.3 %collective-permute-start.1 = (bf16[6,64,1024]{2,1,0:T(8,128)(2,1)S(1)}, bf16[6,64,1024]{2,1,0:T(8,128)(2,1)S(1)}, u32[]{:S(2)}, u32[]{:S(2)}) collective-permute-start(bf16[6,64,1024]{2,1,0:T(8,128)(2,1)S(1)} %pad_maximum_fusion.1), channel_id=1, source_target_pairs={{1,0},{2,1},{3,2},{4,3},{5,4},{6,5},{7,6},{9,8},{10,9},{11,10},{12... | collective-permute-start | bytes 2359304 | tf_op jit(solution)/shard_map/ppermute | solution.py:300
  11.1 0.8 broadcast_in_dim_tile.9.bias2_ref
  11.9 0.8 broadcast_in_dim_tile.8.bias1_ref
  12.6 0.7 reverse_bitcast_fusion
  13.3 0.8 copy.28
  14.1 0.8 copy.26
  14.9 0.7 copy.30
  15.6 0.9 copy.33
  16.7 0.8 copy.34
  17.5 1.1 %copy.35 = bf16[128,3,256]{0,2,1:T(8,128)(2,1)S(1)} copy(bf16[128,3,256]{2,0,1:T(8,128)(2,1)} %bitcast.61) | data formatting | bytes 393216 | tf_op jit(solution)/shard_map/transpose | solution.py:269
  18.6 0.8 copy.37.bwd2_ref
  19.4 1.0 pad_bitcast_fusion.3
  20.6 0.8 copy.31
  21.4 1.1 %copy.32 = bf16[128,3,256]{0,2,1:T(8,128)(2,1)S(1)} copy(bf16[128,3,256]{2,0,1:T(8,128)(2,1)} %bitcast.62) | data formatting | bytes 393216 | tf_op jit(solution)/shard_map/transpose | solution.py:269
  22.5 0.8 copy.36.bwd1_ref
  23.3 1.0 pad_bitcast_fusion.7
  24.5 0.8 copy.27
  25.3 1.0 pad_bitcast_fusion.5
  26.5 0.8 copy.29
  27.9 0.7 add_add_fusion
  28.6 0.7 fusion.13
  29.3 0.9 fusion.7
  30.2 2.4 %fusion.2.col_wave_ref = f32[32,1024]{1,0:T(8,128)} fusion(f32[32]{0:T(128)S(1)} %get-tuple-element.35, s32[32]{0:T(128)S(1)} %get-tuple-element.33, s32[1024]{0:T(1024)S(1)} %iota_add_fusion, pred[32]{0:T(512)(128)(4,1)S(1)} %get-tuple-element.29), kind=kLoop, calls=%fused_computation.26 | loop fusion | flops 294912 | bytes 135456 | tf_op jit(solution)/shard_map/sin | solution.py:282
  32.7 1.1 %broadcast_in_dim.16.row_wave_ref = f32[24,32,128]{2,1,0:T(8,128)} broadcast(f32[24,32]{1,0:T(8,128)S(1)} %fusion.7), dimensions={0,1} | broadcast | bytes 396288 | tf_op jit(solution)/shard_map/broadcast_in_dim | solution.py:285
  34.0 26.1 %step.1 = (bf16[16,64,1024]{2,1,0:T(8,128)(2,1)}, f32[128,8,128]{2,1,0:T(8,128)}) custom-call(s32[2]{0:T(128)} %add_convert_fusion.flags_ref, bf16[16,64,1024]{2,1,0:T(8,128)(2,1)} %bitcast.55, bf16[16,64,1024]{2,1,0:T(8,128)(2,1)} %bitcast.56, bf16[6,64,1024]{2,1,0:T(8,128)(2,1)} %copy-done, bf16[6,64,1024]{2,1,0:T(8,128)(2,1)} %copy-done.1, ...), custom_call_target="tpu_custom_call" | custom-call | tf_op jit(solution)/shard_map/step/pallas_call | solution.py:307
  60.0 26.6 %all_to_all.10 = f32[128,8,128]{2,1,0:T(8,128)S(1)} all-to-all(f32[128,8,128]{2,1,0:T(8,128)} %get-tuple-element.12), channel_id=1, replica_groups=mesh['dp'=16,'space'=8] {'dp','space'}, dimensions={0} | all-to-all | bytes 1048576 | tf_op jit(solution)/shard_map/all_to_all | solution.py:343
  86.8 18.0 %all_to_all.11.full_ref = f32[128,8,128]{2,1,0:T(8,128)} all-to-all(f32[128,8,128]{2,1,0:T(8,128)S(1)} %broadcast_in_dim.18), channel_id=1, replica_groups=mesh['dp'=16,'space'=8] {'dp','space'}, dimensions={0} | all-to-all | bytes 1048576 | tf_op jit(solution)/shard_map/all_to_all | solution.py:345
  104.8 2.0 %split.1 = (f32[3,3,64,64]{3,2,1,0:T(8,128)}, f32[8,64]{1,0:T(8,128)}, f32[3,3,64,64]{3,2,1,0:T(8,128)}, f32[8,64]{1,0:T(8,128)}) custom-call(f32[128,8,128]{2,1,0:T(8,128)} %all_to_all.11.full_ref), custom_call_target="tpu_custom_call" | custom-call | tf_op jit(solution)/shard_map/split/pallas_call | solution.py:348
  106.8 1.2 %slice_bitcast_fusion.4 = (f32[64]{0:T(128)}, f32[64]{0:T(128)}) fusion(f32[8,64]{1,0:T(8,128)} %get-tuple-element.16, f32[8,64]{1,0:T(8,128)} %get-tuple-element.14), kind=kLoop, calls=%fused_computation.45 | loop fusion | bytes 1024 | tf_op jit(solution)/shard_map/squeeze | solution.py:360
  (35 shorter events, 3.9 us)
Async XLA Ops:
  3.0 6.9 %copy-start.4 = (s32[1,2]{1,0:T(1,128)S(1)}, s32[1,2]{1,0:T(1,128)}, u32[]{:S(2)}) copy-start(s32[1,2]{1,0:T(1,128)} %param.9) | copy-start | bytes 28
  3.0 8.1 %copy-start.5 = (f32[64]{0:T(128)S(1)}, f32[64]{0:T(128)}, u32[]{:S(2)}) copy-start(f32[64]{0:T(128)} %param.13) | copy-start | bytes 772
  3.0 8.9 %copy-start.6 = (f32[64]{0:T(128)S(1)}, f32[64]{0:T(128)}, u32[]{:S(2)}) copy-start(f32[64]{0:T(128)} %param.11) | copy-start | bytes 772
  3.0 9.6 %copy-start.2 = (bf16[3,3,64,64]{3,2,1,0:T(8,128)(2,1)S(1)}, bf16[3,3,64,64]{3,2,1,0:T(8,128)(2,1)}, u32[]{:S(2)}) copy-start(bf16[3,3,64,64]{3,2,1,0:T(8,128)(2,1)} %param.12) | copy-start | bytes 221188
  3.0 11.1 %copy-start.3 = (bf16[3,3,64,64]{3,2,1,0:T(8,128)(2,1)S(1)}, bf16[3,3,64,64]{3,2,1,0:T(8,128)(2,1)}, u32[]{:S(2)}) copy-start(bf16[3,3,64,64]{3,2,1,0:T(8,128)(2,1)} %param.10) | copy-start | bytes 221188
  3.1 29.6 %collective-permute-start = (bf16[6,64,1024]{2,1,0:T(8,128)(2,1)S(1)}, bf16[6,64,1024]{2,1,0:T(8,128)(2,1)S(1)}, u32[]{:S(2)}, u32[]{:S(2)}) collective-permute-start(bf16[6,64,1024]{2,1,0:T(8,128)(2,1)S(1)} %pad_maximum_fusion), channel_id=1, source_target_pairs={{0,1},{1,2},{2,3},{3,4},{4,5},{5,6},{6,7},{8,9},{9,10},{10,11},{11... | collective-permute-start | bytes 2359304 | tf_op jit(solution)/shard_map/ppermute | solution.py:297
  7.4 25.3 %collective-permute-start.1 = (bf16[6,64,1024]{2,1,0:T(8,128)(2,1)S(1)}, bf16[6,64,1024]{2,1,0:T(8,128)(2,1)S(1)}, u32[]{:S(2)}, u32[]{:S(2)}) collective-permute-start(bf16[6,64,1024]{2,1,0:T(8,128)(2,1)S(1)} %pad_maximum_fusion.1), channel_id=1, source_target_pairs={{1,0},{2,1},{3,2},{4,3},{5,4},{6,5},{7,6},{9,8},{10,9},{11,10},{12... | collective-permute-start | bytes 2359304 | tf_op jit(solution)/shard_map/ppermute | solution.py:300
  32.7 1.1 %copy-start = (bf16[6,64,1024]{2,1,0:T(8,128)(2,1)}, bf16[6,64,1024]{2,1,0:T(8,128)(2,1)S(1)}, u32[]{:S(2)}) copy-start(bf16[6,64,1024]{2,1,0:T(8,128)(2,1)S(1)} %collective-permute-done.top_ref) | copy-start | bytes 2359300
  32.7 1.3 %copy-start.1 = (bf16[6,64,1024]{2,1,0:T(8,128)(2,1)}, bf16[6,64,1024]{2,1,0:T(8,128)(2,1)S(1)}, u32[]{:S(2)}) copy-start(bf16[6,64,1024]{2,1,0:T(8,128)(2,1)S(1)} %collective-permute-done.1.bot_ref) | copy-start | bytes 2359300

commit v2 on v1

v2 whole, which is shorter than its diff:
```python
import functools
import math

import jax
import jax.numpy as jnp
from jax import lax
from jax.experimental import pallas as pl
from jax.experimental.pallas import tpu as pltpu
from jax.sharding import PartitionSpec as P

BF = jnp.bfloat16
F32 = jnp.float32
AXES = ("dp", "space")
FEAT_HALO = 4
GOAL_HALO = 2
GELU_SCALE = math.sqrt(2.0 / math.pi)
GELU_CUBE = 0.044715


def to_right(value):
    lane = lax.broadcasted_iota(jnp.int32, value.shape, 1)
    return jnp.where(lane == 0, jnp.zeros_like(value), pltpu.roll(value, 1, 1))


def to_left(value):
    last = value.shape[1] - 1
    lane = lax.broadcasted_iota(jnp.int32, value.shape, 1)
    return jnp.where(lane == last, jnp.zeros_like(value), pltpu.roll(value, last, 1))


def keep(flag, value):
    return jnp.where(flag > 0, value, jnp.zeros_like(value))


def masked(value, low, high):
    if low is None and high is None:
        return value
    half = value.shape[0] // 2
    first, second = value[:half], value[half:]
    if low is not None:
        first = keep(low, first)
    if high is not None:
        second = keep(high, second)
    return jnp.concatenate([first, second], axis=0)


def lane_sum(value):
    half = value.shape[0] // 2
    both = value[:half] + value[half:]
    total = both[:, :128]
    for start in range(128, both.shape[1], 128):
        total = total + both[:, start : start + 128]
    return total


def wave(position, channel):
    period = jnp.left_shift(jnp.full_like(channel, 4), channel & 7)
    phase = (position & (period - 1)).astype(F32)
    return jnp.sin(phase * ((2.0 * math.pi) / period.astype(F32)))


def row_waves(anchors_ref, start, half):
    shape = (half, 128)
    lane = lax.broadcasted_iota(jnp.int32, shape, 1)
    channel = lax.broadcasted_iota(jnp.int32, shape, 0)
    return wave(anchors_ref[0, 0] + start + lane, channel)


def col_waves(anchors_ref, half, cols):
    shape = (half, cols)
    lane = lax.broadcasted_iota(jnp.int32, shape, 1)
    channel = lax.broadcasted_iota(jnp.int32, shape, 0)
    return wave(anchors_ref[0, 1] + lane, channel)


def with_geo(value, row_wave, col_wave):
    rows = jnp.broadcast_to(row_wave, col_wave.shape)
    return value.astype(F32) + jnp.concatenate([rows, col_wave], axis=0)


def bias_tile(bias_ref):
    ch = bias_ref.shape[1]
    tile = jnp.transpose(jnp.broadcast_to(bias_ref[...], (128, ch)))
    return jnp.concatenate([tile, tile], axis=0)


def spread(matrix, block, mirrored=False):
    parts = jnp.dot(matrix, block, preferred_element_type=F32)
    pair = parts.shape[0] // 3
    left, right = (to_left, to_right) if mirrored else (to_right, to_left)
    return parts[pair : 2 * pair] + left(parts[:pair]) + right(parts[2 * pair :])


def activate(pre):
    square = pre * pre
    bent = jnp.tanh(pre * (GELU_SCALE + (GELU_SCALE * GELU_CUBE) * square))
    cdf = 0.5 + 0.5 * bent
    inner = GELU_SCALE + (3.0 * GELU_SCALE * GELU_CUBE) * square
    return pre * cdf, cdf + (0.5 * pre) * ((1.0 - bent * bent) * inner)


class Stage:
    def __init__(self, ch, cols):
        self.ch, self.cols = ch, cols

    def rows(self, at, count):
        return slice(at * self.ch, (at + count) * self.ch)

    def wide(self, tile):
        return jnp.tile(tile, (1, self.cols // 128))

    def put_three(self, target, at, value):
        spot = self.rows(at, 2)
        target[0, spot] = to_left(value)
        target[1, spot] = value
        target[2, spot] = to_right(value)

    def forward_one(self, matrix, bias, first, at, hidden, to, deriv=None, d_to=0, low=None, high=None):
        pre = spread(matrix[...], first[self.rows(at, 4)]) + self.wide(bias)
        value, grad = activate(pre)
        hidden[self.rows(to, 2)] = masked(value, low, high).astype(BF)
        if deriv is not None:
            deriv[self.rows(d_to, 2)] = grad

    def forward_two(self, matrix, bias, hidden, at, goal, misfit, to, total, flag=None):
        out = spread(matrix[...], hidden[self.rows(at, 4)]) + self.wide(bias)
        error = out - goal.astype(F32)
        if flag is not None:
            error = keep(flag, error)
        error = error.astype(BF)
        self.put_three(misfit, to, error)
        if flag is None:
            total[...] += lane_sum(error.astype(F32))

    def back(self, matrix, source, at):
        spot = self.rows(at, 4)
        stack = jnp.concatenate([source[0, spot], source[1, spot], source[2, spot]], axis=0)
        return jnp.dot(matrix[...], stack, preferred_element_type=F32)

    def backward_two(self, matrix, misfit, at, deriv, d_at, slope, to, total, low=None, high=None):
        value = self.back(matrix, misfit, at) * deriv[self.rows(d_at, 2)]
        value = masked(value, low, high).astype(BF)
        self.put_three(slope, to, value)
        wide = value.astype(F32)
        ch = self.ch
        if low is not None:
            wide = jnp.concatenate([jnp.zeros_like(wide[:ch]), wide[ch:]], axis=0)
        if high is not None:
            wide = jnp.concatenate([wide[:ch], jnp.zeros_like(wide[ch:])], axis=0)
        total[...] += lane_sum(wide)

    def weight_grad(self, acc, errors, e_at, source, at):
        spot = self.rows(e_at, 2)
        stack = jnp.concatenate([errors[0, spot], errors[1, spot], errors[2, spot]], axis=0)
        acc[...] += lax.dot_general(
            stack,
            source[self.rows(at, 4)],
            (((1,), (1,)), ((), ())),
            preferred_element_type=F32,
        )


def banded(blocks):
    flat = jnp.concatenate(blocks, axis=1)
    gap = jnp.zeros(blocks[0].shape, flat.dtype)
    return jnp.concatenate(
        [jnp.concatenate([flat, gap], axis=1), jnp.concatenate([gap, flat], axis=1)], axis=0
    )


def forward_band(w_ref, j):
    return banded([w_ref[i, j].astype(F32) for i in range(3)]).astype(BF)


def backward_band(w_ref, j):
    return banded([jnp.transpose(w_ref[2 - i, j].astype(F32)) for i in range(3)]).astype(BF)


def inner_kernel(
    rows,
    anchors_ref,
    w1_ref,
    w2_ref,
    b1_ref,
    b2_ref,
    feat_hbm,
    goal_hbm,
    back_hbm,
    first_edge,
    hidden_edge,
    deriv_edge,
    misfit_edge,
    slope_edge,
    fwd1,
    fwd2,
    bwd2,
    bwd1_spread,
    biases,
    col_wave_ref,
    acc1,
    acc2,
    sum1,
    sum2,
    feat,
    goal,
    first,
    hidden,
    deriv,
    misfit,
    slope,
    bwd1,
    back,
    in_sems,
    out_sems,
):
    ch, cols = feat.shape[1:]
    half, pair = ch // 2, 2 * ch
    me = lax.axis_index("space")
    do = Stage(ch, cols)
    loads = [
        pltpu.make_async_copy(feat_hbm.at[k : k + 4], feat.at[k : k + 4], in_sems.at[k // 4])
        for k in range(0, rows, 4)
    ]
    goal_load = pltpu.make_async_copy(goal_hbm, goal, in_sems.at[rows // 4])
    for load in loads:
        load.start()
    goal_load.start()
    for j in range(3):
        spot = slice(pair * j, pair * (j + 1))
        fwd1[spot] = forward_band(w1_ref, j)
        fwd2[spot] = forward_band(w2_ref, j)
        band = backward_band(w1_ref, j)
        bwd1_spread[spot] = band
        bwd1[:, 4 * ch * j : 4 * ch * (j + 1)] = band
        bwd2[:, 4 * ch * j : 4 * ch * (j + 1)] = backward_band(w2_ref, j)
    biases[0] = bias_tile(b1_ref)
    biases[1] = bias_tile(b2_ref)
    row_wave = row_waves(anchors_ref, me * rows, half)
    col_wave_ref[...] = col_waves(anchors_ref, half, cols)
    for total in (acc1, acc2, sum1, sum2):
        total[...] = jnp.zeros_like(total)
    for row in range(rows):
        if row % 4 == 0:
            loads[row // 4].wait()
        first[do.rows(row, 1)] = with_geo(
            feat[row], row_wave[:, row : row + 1], col_wave_ref[...]
        ).astype(BF)
    sends = []

    def send(source, target):
        copy = pltpu.make_async_copy(source, target, out_sems.at[len(sends)])
        copy.start()
        sends.append(copy)

    send(first.at[do.rows(0, 5)], first_edge.at[0])
    send(first.at[do.rows(rows - 5, 5)], first_edge.at[1])
    for r in range(1, rows - 2, 2):
        do.forward_one(fwd1, biases[0], first, r - 1, hidden, r - 1, deriv, r - 1)
    for side, r in enumerate((1, rows - 3)):
        send(hidden.at[do.rows(r - 1, 2)], hidden_edge.at[side])
        send(deriv.at[do.rows(r - 1, 2)], deriv_edge.at[side])
    goal_load.wait()
    for r in range(2, rows - 3, 2):
        goals = jnp.concatenate([goal[r], goal[r + 1]], axis=0)
        do.forward_two(fwd2, biases[1], hidden, r - 2, goals, misfit, r - 2, sum2)
        do.weight_grad(acc2, misfit, r - 2, hidden, r - 2)
    for side, r in enumerate((2, rows - 4)):
        send(misfit.at[:, do.rows(r - 2, 2)], misfit_edge.at[side])
    for r in range(3, rows - 4, 2):
        do.backward_two(bwd2, misfit, r - 3, deriv, r - 1, slope, r - 3, sum1)
    for side, r in enumerate((3, rows - 5)):
        send(slope.at[:, do.rows(r - 3, 2)], slope_edge.at[side])
    for r in range(4, rows - 5, 2):
        do.weight_grad(acc1, slope, r - 3, first, r - 1)
        value = do.back(bwd1, slope, r - 4).astype(BF)
        back[r - 4] = value[:ch]
        back[r - 3] = value[ch:]
    send(back, back_hbm.at[4 : rows - 4])
    for copy in sends:
        copy.wait()


def edge_kernel(
    rows,
    size,
    factor,
    anchors_ref,
    fwd1,
    fwd2,
    bwd2,
    biases,
    col_wave_ref,
    old1,
    old2,
    old_sum1,
    old_sum2,
    goal_hbm,
    even_hbm,
    odd_hbm,
    first_edge,
    hidden_edge,
    deriv_edge,
    misfit_edge,
    slope_edge,
    grads_ref,
    slope_out,
    halo,
    goal,
    first,
    hidden,
    deriv,
    misfit,
    slope,
    acc1,
    acc2,
    sum1,
    sum2,
    halo_sems,
    in_sems,
    out_sems,
):
    ch, cols = goal.shape[2:]
    half = ch // 2
    me = lax.axis_index("space")
    above = (me > 0).astype(jnp.int32)
    below = (me < size - 1).astype(jnp.int32)
    odd = lax.rem(me, 2)
    do = Stage(ch, cols)
    for side in range(2):

        @pl.when(odd == side)
        def _():
            pltpu.make_async_copy(odd_hbm, halo.at[side], halo_sems.at[side]).start()

        @pl.when(odd != side)
        def _():
            pltpu.make_async_copy(even_hbm, halo.at[side], halo_sems.at[side]).start()

    places = (
        (first_edge, first, (4, 0), 5, False),
        (hidden_edge, hidden, (4, 0), 2, False),
        (deriv_edge, deriv, (2, 0), 2, False),
        (misfit_edge, misfit, (4, 0), 2, True),
        (slope_edge, slope, (4, 0), 2, True),
    )
    loads = []

    def load(source, target):
        copy = pltpu.make_async_copy(source, target, in_sems.at[len(loads)])
        copy.start()
        loads.append(copy)

    for source, target, spots, count, three in places:
        for side in range(2):
            spot = do.rows(spots[side], count)
            load(
                source.at[side],
                target.at[side, :, spot] if three else target.at[side, spot],
            )
    for side, r in enumerate((0, rows - 2)):
        load(goal_hbm.at[r : r + 2], goal.at[side])
    acc1[...] = old1[...]
    acc2[...] = old2[...]
    sum1[...] = old_sum1[...]
    sum2[...] = old_sum2[...]
    flags = (above, below)
    for side in range(2):
        pltpu.make_async_copy(even_hbm, halo.at[side], halo_sems.at[side]).wait()
    for side, (start, to) in enumerate(((-4, 0), (rows, 5))):
        row_wave = row_waves(anchors_ref, me * rows + start, half)
        for k in range(4):
            value = with_geo(halo[side, k], row_wave[:, k : k + 1], col_wave_ref[...])
            first[side, do.rows(to + k, 1)] = keep(flags[side], value).astype(BF)
    for copy in loads:
        copy.wait()
    top, low = 0, 1
    F, H, D, M, S = ([ref.at[0], ref.at[1]] for ref in (first, hidden, deriv, misfit, slope))
    one = functools.partial(do.forward_one, fwd1, biases[0])
    one(F[top], 0, H[top], 0, low=above, high=above)
    one(F[low], 5, H[low], 4, low=below, high=below)
    one(F[top], 2, H[top], 2, D[top], 0, low=above)
    one(F[low], 3, H[low], 2, D[low], 2, high=below)

    def goals(ref, side, at):
        return jnp.concatenate([ref[side, at], ref[side, at + 1]], axis=0)

    two = functools.partial(do.forward_two, fwd2, biases[1])
    two(H[top], 0, goals(halo, 0, 4), M[top], 0, sum2, flag=above)
    two(H[low], 2, goals(halo, 1, 4), M[low], 4, sum2, flag=below)
    two(H[top], 2, goals(goal, 0, 0), M[top], 2, sum2)
    two(H[low], 0, goals(goal, 1, 0), M[low], 2, sum2)
    do.weight_grad(acc2, M[top], 2, H[top], 2)
    do.weight_grad(acc2, M[low], 2, H[low], 0)
    bend = functools.partial(do.backward_two, bwd2)
    bend(M[top], 0, D[top], 0, S[top], 0, sum1, low=above)
    bend(M[low], 2, D[low], 2, S[low], 4, sum1, high=below)
    bend(M[top], 2, D[top], 2, S[top], 2, sum1)
    bend(M[low], 0, D[low], 0, S[low], 2, sum1)
    sends = [
        pltpu.make_async_copy(slope.at[side, 1], slope_out.at[side], out_sems.at[side])
        for side in range(2)
    ]
    for copy in sends:
        copy.start()
    do.weight_grad(acc1, S[top], 1, F[top], 3)
    do.weight_grad(acc1, S[low], 1, F[low], 0)
    do.weight_grad(acc1, S[top], 3, F[top], 5)
    do.weight_grad(acc1, S[low], 3, F[low], 2)

    def emit(base, acc, total):
        summed = jnp.sum(total[...], axis=1, keepdims=True)
        side = jnp.broadcast_to(summed, (ch, ch))
        for j in range(3):
            upper = acc[2 * j * ch : (2 * j + 1) * ch]
            lower = acc[(2 * j + 1) * ch : (2 * j + 2) * ch]
            block = jnp.concatenate([upper[:, : 3 * ch] + lower[:, ch:], side], axis=1) * factor
            for t in range(ch // 8):
                for part in range(2):
                    grads_ref[base + (j * (ch // 8) + t) * 2 + part] = block[
                        8 * t : 8 * t + 8, 128 * part : 128 * part + 128
                    ]

    emit(0, acc1, sum1)
    emit(6 * (ch // 8), acc2, sum2)
    for spare in range(12 * (ch // 8), grads_ref.shape[0]):
        grads_ref[spare] = jnp.zeros((8, 128), F32)
    for copy in sends:
        copy.wait()


def rest_kernel(rows, old_back, bwd1_spread, slope, back_hbm, back, sems):
    ch = back.shape[2]
    do = Stage(ch, back.shape[3])
    sends = []
    for at in range(2):
        for side in range(2):
            block = slope[side, do.rows(2 * at, 4)]
            value = spread(bwd1_spread[...], block, mirrored=True).astype(BF)
            back[side, 2 * at] = value[:ch]
            back[side, 2 * at + 1] = value[ch:]
    for side, r in enumerate((0, rows - 4)):
        copy = pltpu.make_async_copy(back.at[side], back_hbm.at[r : r + 4], sems.at[side])
        copy.start()
        sends.append(copy)
    for copy in sends:
        copy.wait()


def split_kernel(ch, full_ref, w1_ref, b1_ref, w2_ref, b2_ref):
    for base, w_ref, b_ref in ((0, w1_ref, b1_ref), (6 * (ch // 8), w2_ref, b2_ref)):
        for j in range(3):
            left, right = [
                jnp.concatenate(
                    [
                        full_ref[base + (j * (ch // 8) + t) * 2 + part].astype(F32)
                        for t in range(ch // 8)
                    ],
                    axis=0,
                )
                for part in range(2)
            ]
            w_ref[0, j] = left[:, :ch]
            w_ref[1, j] = left[:, ch:]
            w_ref[2, j] = right[:, :ch]
            if j == 0:
                b_ref[...] = jnp.transpose(right)[ch : ch + 1]


def shards(features, target, anchors, w_first, b_first, w_second, b_second):
    _, rows, ch, cols = features.shape
    size = lax.axis_size("space")
    devices = size * lax.axis_size("dp")
    me = lax.axis_index("space")
    factor = 1.0 / math.sqrt(features.shape[0] * devices * rows * cols)
    feats, goals = features[0], target[0]
    pair, quad = 2 * ch, 4 * ch

    def edge(wants_bottom):
        start = jnp.where(wants_bottom, rows - FEAT_HALO, 0)
        goal_start = jnp.where(wants_bottom, rows - GOAL_HALO, 0)
        return jnp.concatenate(
            [
                lax.dynamic_slice_in_dim(feats, start, FEAT_HALO),
                lax.dynamic_slice_in_dim(goals, goal_start, GOAL_HALO),
            ]
        )

    is_even = lax.rem(me, 2) == 0
    links = [
        [
            link
            for low in range(first, size - 1, 2)
            for link in ((low, low + 1), (low + 1, low))
        ]
        for first in (0, 1)
    ]
    even_halo = lax.ppermute(edge(is_even), "space", links[0])
    odd_halo = lax.ppermute(edge(jnp.logical_not(is_even)), "space", links[1])

    vmem = pl.BlockSpec(memory_space=pltpu.VMEM)
    smem = pl.BlockSpec(memory_space=pltpu.SMEM)
    anywhere = pl.BlockSpec(memory_space=pl.ANY)

    def shape(*dims, dtype=BF):
        return jax.ShapeDtypeStruct(dims, dtype)

    def buffer(count, *lead, dtype=BF):
        return pltpu.VMEM(lead + (count * ch, cols), dtype)

    (
        back,
        first_edge,
        hidden_edge,
        deriv_edge,
        misfit_edge,
        slope_edge,
        fwd1,
        fwd2,
        bwd2,
        bwd1_spread,
        biases,
        col_wave,
        acc1,
        acc2,
        sum1,
        sum2,
    ) = pl.pallas_call(
        functools.partial(inner_kernel, rows),
        out_shape=(
            shape(rows, ch, cols),
            shape(2, 5 * ch, cols),
            shape(2, pair, cols),
            shape(2, pair, cols, dtype=F32),
            shape(2, 3, pair, cols),
            shape(2, 3, pair, cols),
            shape(3 * pair, quad),
            shape(3 * pair, quad),
            shape(pair, 3 * quad),
            shape(3 * pair, quad),
            shape(2, pair, 128, dtype=F32),
            shape(ch // 2, cols, dtype=F32),
            shape(3 * pair, quad, dtype=F32),
            shape(3 * pair, quad, dtype=F32),
            shape(ch, 128, dtype=F32),
            shape(ch, 128, dtype=F32),
        ),
        in_specs=[smem] + [vmem] * 4 + [anywhere] * 2,
        out_specs=(anywhere,) * 6 + (vmem,) * 10,
        scratch_shapes=[
            pltpu.VMEM((rows, ch, cols), BF),
            pltpu.VMEM((rows, ch, cols), BF),
            buffer(rows),
            buffer(rows - 2),
            buffer(rows - 2, dtype=F32),
            buffer(rows - 4, 3),
            buffer(rows - 6, 3),
            pltpu.VMEM((pair, 3 * quad), BF),
            pltpu.VMEM((rows - 8, ch, cols), BF),
            pltpu.SemaphoreType.DMA((rows // 4 + 1,)),
            pltpu.SemaphoreType.DMA((11,)),
        ],
        compiler_params=pltpu.CompilerParams(vmem_limit_bytes=40 << 20),
        cost_estimate=pl.CostEstimate(
            flops=14 * 10**9, bytes_accessed=12 * 10**6, transcendentals=10**6
        ),
        name="inner",
    )(
        anchors,
        w_first,
        w_second,
        b_first[None],
        b_second[None],
        feats,
        goals,
    )
    grads, slope = pl.pallas_call(
        functools.partial(edge_kernel, rows, size, factor),
        out_shape=(shape(devices, 8, 128, dtype=F32), shape(2, 6 * ch, cols)),
        in_specs=[smem] + [vmem] * 9 + [anywhere] * 8,
        out_specs=(vmem, anywhere),
        scratch_shapes=[
            pltpu.VMEM((2, FEAT_HALO + GOAL_HALO, ch, cols), BF),
            pltpu.VMEM((2, GOAL_HALO, ch, cols), BF),
            buffer(9, 2),
            buffer(6, 2),
            buffer(4, 2, dtype=F32),
            buffer(6, 2, 3),
            buffer(6, 2, 3),
            pltpu.VMEM((3 * pair, quad), F32),
            pltpu.VMEM((3 * pair, quad), F32),
            pltpu.VMEM((ch, 128), F32),
            pltpu.VMEM((ch, 128), F32),
            pltpu.SemaphoreType.DMA((2,)),
            pltpu.SemaphoreType.DMA((12,)),
            pltpu.SemaphoreType.DMA((2,)),
        ],
        compiler_params=pltpu.CompilerParams(vmem_limit_bytes=40 << 20),
        cost_estimate=pl.CostEstimate(
            flops=9 * 10**9, bytes_accessed=10 * 10**6, transcendentals=5 * 10**5
        ),
        name="edges",
    )(
        anchors,
        fwd1,
        fwd2,
        bwd2,
        biases,
        col_wave,
        acc1,
        acc2,
        sum1,
        sum2,
        goals,
        even_halo,
        odd_halo,
        first_edge,
        hidden_edge,
        deriv_edge,
        misfit_edge,
        slope_edge,
    )
    parts = lax.all_to_all(grads, AXES, 0, 0, tiled=True)
    back = pl.pallas_call(
        functools.partial(rest_kernel, rows),
        out_shape=shape(rows, ch, cols),
        in_specs=[anywhere, vmem, vmem],
        out_specs=anywhere,
        scratch_shapes=[
            pltpu.VMEM((2, 4, ch, cols), BF),
            pltpu.SemaphoreType.DMA((2,)),
        ],
        input_output_aliases={0: 0},
        compiler_params=pltpu.CompilerParams(vmem_limit_bytes=20 << 20),
        cost_estimate=pl.CostEstimate(
            flops=2 * 10**9, bytes_accessed=3 * 10**6, transcendentals=0
        ),
        name="rest",
    )(back, bwd1_spread, slope)
    mine = jnp.sum(parts, axis=0).astype(BF)
    full = lax.all_to_all(
        jnp.broadcast_to(mine[None], (devices, 8, 128)), AXES, 0, 0, tiled=True
    )
    grad_w1, grad_b1, grad_w2, grad_b2 = pl.pallas_call(
        functools.partial(split_kernel, ch),
        out_shape=(
            shape(3, 3, ch, ch, dtype=F32),
            shape(1, ch, dtype=F32),
            shape(3, 3, ch, ch, dtype=F32),
            shape(1, ch, dtype=F32),
        ),
        in_specs=[vmem],
        out_specs=(vmem,) * 4,
        name="split",
    )(full)
    return (back[None], grad_w1, grad_b1[0], grad_w2, grad_b2[0])


def solution(mesh):
    in_specs = (
        P("dp", "space", None, None),
        P("dp", "space", None, None),
        P("dp", None),
        P(),
        P(),
        P(),
        P(),
    )
    out_specs = (P("dp", "space", None, None), P(), P(), P(), P())
    return jax.shard_map(shards, mesh=mesh, in_specs=in_specs, out_specs=out_specs, check_vma=False)
```

time: 108 us -> 80.9 us (0.75)
  local copies, waits for them, and re-layouts: 22 us -> 3.98 us
  blocking collectives: 44.6 us -> 29 us
  waiting for transfers between devices: 0.01 us -> 8.7 us
  other arithmetic: 7.04 us -> 0.28 us
  Pallas kernels: 28 us -> 30.6 us
  starting transfers between devices: 5.49 us -> 7.32 us
    all_to_all x1 -> x0, blocking collectives: 18 us -> none  [shards(): lax.all_to_all(jnp.broadcast_to(mine[None], (devices, 8, 128)), AXES, 0,...]
    all_to_all x0 -> x1, waiting for transfers between devices: none -> 8.7 us  [shards(): lax.all_to_all(jnp.broadcast_to(mine[None], (devices, 8, 128)), AXES, 0,...]
    another operation x12 -> x0, local copies, waits for them, and re-layouts: 8.08 us -> none  [the longest x8 6.56 us: pair_matrix(): return jnp.stack([low, high], axis=1).reshape(3, 2 * ch, 4 * ch)]
    transpose x8 -> x0, local copies, waits for them, and re-layouts: 6.02 us -> none  [the longest x6 3.85 us: pair_matrix(): flat = jnp.transpose(kernel, order).reshape(3, ch, 3 * ch)]
    all_to_all x0 -> x1, starting transfers between devices: none -> 4.42 us  [shards(): lax.all_to_all(jnp.broadcast_to(mine[None], (devices, 8, 128)), AXES, 0,...]
    slice x4 -> x0, local copies, waits for them, and re-layouts: 3.64 us -> none  [the longest x1 1.27 us: shards(): feats[:FEAT_HALO]]
    sin x2 -> x0, other arithmetic: 3.36 us -> none  [the longest x1 2.43 us: waves(): jnp.sin(jnp.remainder(col_pos, periods[half:, None]).astype(F32) * scaled...]
    ppermute x2, starting transfers between devices: 5.49 us -> 2.9 us  [the longest x1 2.19 us: shards(): even_halo = lax.ppermute(edge(is_even), 'space', links[0])]
  transfers between devices with their start and end apart: 2 -> 3, of which waited for: 0 -> 1; matrix products, arithmetic and copies ran while one was open for 22% -> 0% of each run, Pallas kernels for 0% -> 23%
where the time goes in v2:
time: 80.9 us; the launch traced here: 80.7 us
  Pallas kernels  30.6 us (38%)
  blocking collectives  29 us (36%)
  waiting for transfers between devices  8.7 us (11%)
  starting transfers between devices  7.32 us (9%)
  local copies, waits for them, and re-layouts  3.98 us (5%)
  between operations  0.83 us (1%)
    all_to_all x1, blocking collectives, shards(): parts = lax.all_to_all(grads, AXES, 0, 0, tiled=True)  29 us
    pallas_call x1, Pallas kernels, shards(): pl.pallas_call(functools.partial(inner_kernel, rows), out_shape=(shape(ro...  16.6 us
    pallas_call x1, Pallas kernels, shards(): pl.pallas_call(functools.partial(edge_kernel, rows, size, factor), out_sh...  9.78 us
    all_to_all x1, waiting for transfers between devices, shards(): lax.all_to_all(jnp.broadcast_to(mine[None], (devices, 8, 128)), AXES, 0,...  8.7 us
    all_to_all x1, starting transfers between devices, shards(): lax.all_to_all(jnp.broadcast_to(mine[None], (devices, 8, 128)), AXES, 0,...  4.42 us
    pallas_call x1, Pallas kernels, shards(): pl.pallas_call(functools.partial(rest_kernel, rows), out_shape=shape(rows...  2.38 us
    ppermute x1, starting transfers between devices, shards(): even_halo = lax.ppermute(edge(is_even), 'space', links[0])  2.19 us
    pallas_call x1, Pallas kernels, shards(): pl.pallas_call(functools.partial(split_kernel, ch), out_shape=(shape(3, 3...  1.88 us
  transfers between devices with their start and end apart: 3, of which 1 were waited for; matrix products, arithmetic and copies ran while one was open for 0% of the time, Pallas kernels for 23%

profile of v2, /device:TPU:1, one launch (start us, length us, event | category | flops | bytes accessed | tf_op | source)
XLA Modules:
  0.0 80.7 jit_solution(16580919458982217451)
XLA Ops:
  0.6 1.1 %dynamic-slice_bitcast_fusion.2 = (bf16[2,64,1024]{2,1,0:T(8,128)(2,1)S(1)}, bf16[2,64,1024]{2,1,0:T(8,128)(2,1)S(1)}) fusion(bf16[1,16,64,1024]{3,2,1,0:T(8,128)(2,1)} %param.8, s32[]{:T(128)S(6)} %select_n.20, s32[]{:T(128)S(6)} %select_n.18), kind=kLoop, calls=%fused_computation.4 | loop fusion | bytes 1048584 | tf_op jit(solution)/shard_map/dynamic_slice | solution.py:484
  1.7 0.0 copy-start.1
  1.7 1.4 %dynamic-slice_bitcast_fusion = (bf16[4,64,1024]{2,1,0:T(8,128)(2,1)S(1)}, bf16[4,64,1024]{2,1,0:T(8,128)(2,1)S(1)}) fusion(bf16[1,16,64,1024]{3,2,1,0:T(8,128)(2,1)} %param.7, s32[]{:T(128)S(6)} %select_n.19, s32[]{:T(128)S(6)} %select_n.17), kind=kLoop, calls=%fused_computation.2 | loop fusion | bytes 2097160 | tf_op jit(solution)/shard_map/dynamic_slice | solution.py:483
  3.2 0.0 copy-start
  3.2 0.0 copy-start.2
  3.2 0.0 copy-start.3
  3.2 0.0 copy-start.4
  3.2 0.0 copy-start.5
  3.2 0.0 copy-start.6
  3.2 0.1 pad_maximum_fusion
  3.3 2.2 %collective-permute-start = (bf16[6,64,1024]{2,1,0:T(8,128)(2,1)S(1)}, bf16[6,64,1024]{2,1,0:T(8,128)(2,1)S(1)}, u32[]{:S(2)}, u32[]{:S(2)}) collective-permute-start(bf16[6,64,1024]{2,1,0:T(8,128)(2,1)S(1)} %pad_maximum_fusion), channel_id=1, source_target_pairs={{0,1},{1,0},{2,3},{3,2},{4,5},{5,4},{6,7},{7,6},{8,9},{9,8},{10,11... | collective-permute-start | bytes 2359304 | tf_op jit(solution)/shard_map/ppermute | solution.py:497
  5.5 0.1 pad_maximum_fusion.1
  5.6 0.7 collective-permute-start.1
  6.3 0.0 copy-done.1
  6.3 0.0 copy-done
  6.3 0.0 copy-done.2
  6.3 0.0 copy-done.3
  6.3 0.0 copy-done.4
  6.3 0.0 copy-done.5
  6.4 0.0 copy-done.6
  6.4 16.6 %inner.1 = (bf16[16,64,1024]{2,1,0:T(8,128)(2,1)}, bf16[2,320,1024]{2,1,0:T(8,128)(2,1)S(1)}, bf16[2,128,1024]{2,1,0:T(8,128)(2,1)S(1)}, f32[2,128,1024]{2,1,0:T...) custom-call(s32[1,2]{1,0:T(1,128)S(1)} %copy-done.6, ...), custom_call_target="tpu_custom_call" | custom-call | flops 14000000000 | bytes 12000000 | tf_op jit(solution)/shard_map/inner/pallas_call | solution.py:527
  22.9 0.0 collective-permute-done.even_hbm
  23.0 0.0 collective-permute-done.1.odd_hbm
  23.0 9.8 %edges.1 = (f32[128,8,128]{2,1,0:T(8,128)S(1)}, bf16[2,384,1024]{2,1,0:T(8,128)(2,1)S(1)}) custom-call(s32[1,2]{1,0:T(1,128)S(1)} %copy-done.6, bf16[384,256]{1,0:T(8,128)(2,1)S(1)} %get-tuple-element.29.fwd1, bf16[384,256]{1,0:T(8,128)(2,1)S(1)} %get-tuple-element.30.fwd2, bf16[128,768]{1,0:T(8,128)(2,1)S(1)} %get-tuple-element.31.bwd2, ...), custom_call_target="tpu_custom_call" | custom-call | flops 8999999488 | bytes 10000000 | tf_op jit(solution)/shard_map/edges/pallas_call | solution.py:576
  32.7 29.0 %all_to_all.10 = f32[128,8,128]{2,1,0:T(8,128)S(1)} all-to-all(f32[128,8,128]{2,1,0:T(8,128)S(1)} %get-tuple-element.44), channel_id=1, replica_groups=mesh['dp'=16,'space'=8] {'dp','space'}, dimensions={0} | all-to-all | bytes 1048576 | tf_op jit(solution)/shard_map/all_to_all | solution.py:622
  61.7 0.1 reduce_sum.9
  61.9 0.7 broadcast_in_dim.18
  62.6 4.4 %all-to-all-start.1 = ((bf16[128,8,128]{2,1,0:T(8,128)(2,1)}), bf16[128,8,128]{2,1,0:T(8,128)(2,1)S(1)}, u32[]{:S(2)}, u32[]{:S(2)}) async-start(bf16[128,8,128]{2,1,0:T(8,128)(2,1)} %broadcast_in_dim.18), calls=%async_computation.1 | async-start | bytes 524288 | tf_op jit(solution)/shard_map/all_to_all | solution.py:640
  67.0 2.4 %rest.1 = bf16[16,64,1024]{2,1,0:T(8,128)(2,1)} custom-call(bf16[16,64,1024]{2,1,0:T(8,128)(2,1)} %get-tuple-element.27.old_back, bf16[384,256]{1,0:T(8,128)(2,1)S(1)} %get-tuple-element.28.bwd1_spread, bf16[2,384,1024]{2,1,0:T(8,128)(2,1)S(1)} %get-tuple-element.43.slope), custom_call_target="tpu_custom_call", output_to_operand_aliasing={{}: (0, {})} | custom-call | flops 2000000000 | bytes 3000000 | tf_op jit(solution)/shard_map/rest/pallas_call | solution.py:623
  69.4 8.7 %all-to-all-done.1.full_ref = bf16[128,8,128]{2,1,0:T(8,128)(2,1)S(1)} async-done(((bf16[128,8,128]{2,1,0:T(8,128)(2,1)}), bf16[128,8,128]{2,1,0:T(8,128)(2,1)S(1)}, u32[]{:S(2)}, u32[]{:S(2)}) %all-to-all-start.1) | async-done | bytes 262176 | tf_op jit(solution)/shard_map/all_to_all | solution.py:640
  78.1 0.7 copy-done.7
  78.8 1.9 %split.1 = (f32[3,3,64,64]{3,2,1,0:T(8,128)}, f32[1,64]{1,0:T(1,128)}, f32[3,3,64,64]{3,2,1,0:T(8,128)}, f32[1,64]{1,0:T(1,128)}) custom-call(bf16[128,8,128]{2,1,0:T(8,128)(2,1)} %copy-done.7), custom_call_target="tpu_custom_call" | custom-call | tf_op jit(solution)/shard_map/split/pallas_call | solution.py:643
  (1 shorter events, 0.0 us)
Async XLA Ops:
  1.7 4.6 %copy-start.1 = (bf16[1,16,64,1024]{3,2,1,0:T(8,128)(2,1)S(1)}, bf16[1,16,64,1024]{3,2,1,0:T(8,128)(2,1)}, u32[]{:S(2)}) copy-start(bf16[1,16,64,1024]{3,2,1,0:T(8,128)(2,1)} %param.8) | copy-start | bytes 6291460
  3.2 3.1 %copy-start = (bf16[1,16,64,1024]{3,2,1,0:T(8,128)(2,1)S(1)}, bf16[1,16,64,1024]{3,2,1,0:T(8,128)(2,1)}, u32[]{:S(2)}) copy-start(bf16[1,16,64,1024]{3,2,1,0:T(8,128)(2,1)} %param.7) | copy-start | bytes 6291460
  3.2 3.1 %copy-start.2 = (bf16[3,3,64,64]{3,2,1,0:T(8,128)(2,1)S(1)}, bf16[3,3,64,64]{3,2,1,0:T(8,128)(2,1)}, u32[]{:S(2)}) copy-start(bf16[3,3,64,64]{3,2,1,0:T(8,128)(2,1)} %w1_ref.1) | copy-start | bytes 221188
  3.2 3.1 %copy-start.3 = (bf16[3,3,64,64]{3,2,1,0:T(8,128)(2,1)S(1)}, bf16[3,3,64,64]{3,2,1,0:T(8,128)(2,1)}, u32[]{:S(2)}) copy-start(bf16[3,3,64,64]{3,2,1,0:T(8,128)(2,1)} %w2_ref.1) | copy-start | bytes 221188
  3.2 3.1 %copy-start.4 = (f32[64]{0:T(128)S(1)}, f32[64]{0:T(128)}, u32[]{:S(2)}) copy-start(f32[64]{0:T(128)} %param.11) | copy-start | bytes 772
  3.2 3.1 %copy-start.5 = (f32[64]{0:T(128)S(1)}, f32[64]{0:T(128)}, u32[]{:S(2)}) copy-start(f32[64]{0:T(128)} %param.13) | copy-start | bytes 772
  3.2 3.1 %copy-start.6 = (s32[1,2]{1,0:T(1,128)S(1)}, s32[1,2]{1,0:T(1,128)}, u32[]{:S(2)}) copy-start(s32[1,2]{1,0:T(1,128)} %anchors_ref.3) | copy-start | bytes 28
  3.3 19.6 %collective-permute-start = (bf16[6,64,1024]{2,1,0:T(8,128)(2,1)S(1)}, bf16[6,64,1024]{2,1,0:T(8,128)(2,1)S(1)}, u32[]{:S(2)}, u32[]{:S(2)}) collective-permute-start(bf16[6,64,1024]{2,1,0:T(8,128)(2,1)S(1)} %pad_maximum_fusion), channel_id=1, source_target_pairs={{0,1},{1,0},{2,3},{3,2},{4,5},{5,4},{6,7},{7,6},{8,9},{9,8},{10,11... | collective-permute-start | bytes 2359304 | tf_op jit(solution)/shard_map/ppermute | solution.py:497
  5.6 17.4 %collective-permute-start.1 = (bf16[6,64,1024]{2,1,0:T(8,128)(2,1)S(1)}, bf16[6,64,1024]{2,1,0:T(8,128)(2,1)S(1)}, u32[]{:S(2)}, u32[]{:S(2)}) collective-permute-start(bf16[6,64,1024]{2,1,0:T(8,128)(2,1)S(1)} %pad_maximum_fusion.1), channel_id=1, source_target_pairs={{1,2},{2,1},{3,4},{4,3},{5,6},{6,5},{9,10},{10,9},{11,12},{12,11},... | collective-permute-start | bytes 2359304 | tf_op jit(solution)/shard_map/ppermute | solution.py:498
  62.6 15.5 %all-to-all-start.1 = ((bf16[128,8,128]{2,1,0:T(8,128)(2,1)}), bf16[128,8,128]{2,1,0:T(8,128)(2,1)S(1)}, u32[]{:S(2)}, u32[]{:S(2)}) async-start(bf16[128,8,128]{2,1,0:T(8,128)(2,1)} %broadcast_in_dim.18), calls=%async_computation.1 | async-start | bytes 524288 | tf_op jit(solution)/shard_map/all_to_all | solution.py:640
  78.1 0.7 copy-start.7

commit v3 on v2

v3 whole, which is shorter than its diff:
```python
import functools
import math

import jax
import jax.numpy as jnp
from jax import lax
from jax.experimental import pallas as pl
from jax.experimental.pallas import tpu as pltpu
from jax.sharding import PartitionSpec as P

BF = jnp.bfloat16
F32 = jnp.float32
AXES = ("dp", "space")
FEAT_HALO = 4
GOAL_HALO = 2
GELU_SCALE = math.sqrt(2.0 / math.pi)
GELU_CUBE = 0.044715


def to_right(value):
    moved = pltpu.roll(value, 1, 1)
    edge = moved[:, :128]
    lane = lax.broadcasted_iota(jnp.int32, edge.shape, 1)
    edge = jnp.where(lane == 0, jnp.zeros_like(edge), edge)
    return jnp.concatenate([edge, moved[:, 128:]], axis=1)


def to_left(value):
    cols = value.shape[1]
    moved = pltpu.roll(value, cols - 1, 1)
    edge = moved[:, cols - 128 :]
    lane = lax.broadcasted_iota(jnp.int32, edge.shape, 1)
    edge = jnp.where(lane == 127, jnp.zeros_like(edge), edge)
    return jnp.concatenate([moved[:, : cols - 128], edge], axis=1)


def keep(flag, value):
    return jnp.where(flag > 0, value, jnp.zeros_like(value))


def masked(value, low, high):
    if low is None and high is None:
        return value
    half = value.shape[0] // 2
    first, second = value[:half], value[half:]
    if low is not None:
        first = keep(low, first)
    if high is not None:
        second = keep(high, second)
    return jnp.concatenate([first, second], axis=0)


def lane_sum(value):
    half = value.shape[0] // 2
    both = value[:half] + value[half:]
    total = both[:, :128]
    for start in range(128, both.shape[1], 128):
        total = total + both[:, start : start + 128]
    return total


def wave(position, channel):
    period = jnp.left_shift(jnp.full_like(channel, 4), channel & 7)
    phase = (position & (period - 1)).astype(F32)
    return jnp.sin(phase * ((2.0 * math.pi) / period.astype(F32)))


def row_waves(anchors_ref, start, half):
    shape = (half, 128)
    lane = lax.broadcasted_iota(jnp.int32, shape, 1)
    channel = lax.broadcasted_iota(jnp.int32, shape, 0)
    return wave(anchors_ref[0, 0] + start + lane, channel)


def col_waves(anchors_ref, half, cols):
    shape = (half, cols)
    lane = lax.broadcasted_iota(jnp.int32, shape, 1)
    channel = lax.broadcasted_iota(jnp.int32, shape, 0)
    return wave(anchors_ref[0, 1] + lane, channel)


def with_geo(value, row_wave, col_wave):
    rows = jnp.broadcast_to(row_wave, col_wave.shape)
    return value.astype(F32) + jnp.concatenate([rows, col_wave], axis=0)


def bias_tile(bias_ref):
    ch = bias_ref.shape[1]
    tile = jnp.transpose(jnp.broadcast_to(bias_ref[...], (128, ch)))
    return jnp.concatenate([tile, tile], axis=0)


def spread(matrix, block, mirrored=False):
    parts = jnp.dot(matrix, block, preferred_element_type=F32)
    pair = parts.shape[0] // 3
    left, right = (to_left, to_right) if mirrored else (to_right, to_left)
    return parts[pair : 2 * pair] + left(parts[:pair]) + right(parts[2 * pair :])


def activate(pre):
    square = pre * pre
    cdf = 0.5 + 0.5 * jnp.tanh(pre * (GELU_SCALE + (GELU_SCALE * GELU_CUBE) * square))
    value = pre * cdf
    bend = 2.0 * GELU_SCALE + (6.0 * GELU_SCALE * GELU_CUBE) * square
    return value, cdf + value * ((1.0 - cdf) * bend)


def view(*parts):
    def read(at, count, ch, plane=None):
        blocks = []
        for ref, start, rows in parts:
            low, high = max(at, 0), min(at + count, rows)
            if low < high:
                spot = slice((start + low) * ch, (start + high) * ch)
                blocks.append(ref[spot] if plane is None else ref[plane, spot])
            at, count = at - rows, count
        return blocks[0] if len(blocks) == 1 else jnp.concatenate(blocks, axis=0)

    return read


class Stage:
    def __init__(self, ch, cols):
        self.ch, self.cols = ch, cols

    def rows(self, at, count):
        return slice(at * self.ch, (at + count) * self.ch)

    def wide(self, tile):
        return jnp.tile(tile, (1, self.cols // 128))

    def put_three(self, target, at, value):
        spot = self.rows(at, 2)
        target[0, spot] = to_left(value)
        target[1, spot] = value
        target[2, spot] = to_right(value)

    def forward_one(self, matrix, bias, first, at, hidden, to, deriv=None, d_to=0, low=None, high=None):
        pre = spread(matrix[...], first(at, 4, self.ch)) + self.wide(bias)
        value, grad = activate(pre)
        hidden[self.rows(to, 2)] = masked(value, low, high).astype(BF)
        if deriv is not None:
            deriv[self.rows(d_to, 2)] = grad

    def forward_two(self, matrix, bias, hidden, at, goal, misfit, to, total, flag=None):
        out = spread(matrix[...], hidden(at, 4, self.ch)) + self.wide(bias)
        error = out - goal.astype(F32)
        if flag is not None:
            error = keep(flag, error)
        error = error.astype(BF)
        self.put_three(misfit, to, error)
        if flag is None:
            total[...] += lane_sum(error.astype(F32))

    def three(self, source, at, count):
        return jnp.concatenate([source(at, count, self.ch, plane) for plane in range(3)], axis=0)

    def back(self, matrix, source, at):
        return jnp.dot(matrix[...], self.three(source, at, 4), preferred_element_type=F32)

    def backward_two(self, matrix, misfit, at, deriv, d_at, slope, to, total, low=None, high=None):
        value = self.back(matrix, misfit, at) * deriv(d_at, 2, self.ch)
        value = masked(value, low, high).astype(BF)
        self.put_three(slope, to, value)
        wide = value.astype(F32)
        ch = self.ch
        if low is not None:
            wide = jnp.concatenate([jnp.zeros_like(wide[:ch]), wide[ch:]], axis=0)
        if high is not None:
            wide = jnp.concatenate([wide[:ch], jnp.zeros_like(wide[ch:])], axis=0)
        total[...] += lane_sum(wide)

    def weight_grad(self, acc, errors, e_at, source, at):
        acc[...] += lax.dot_general(
            self.three(errors, e_at, 2),
            source(at, 4, self.ch),
            (((1,), (1,)), ((), ())),
            preferred_element_type=F32,
        )


def banded(blocks):
    flat = jnp.concatenate(blocks, axis=1)
    gap = jnp.zeros(blocks[0].shape, flat.dtype)
    return jnp.concatenate(
        [jnp.concatenate([flat, gap], axis=1), jnp.concatenate([gap, flat], axis=1)], axis=0
    )


def forward_band(w_ref, j):
    return banded([w_ref[i, j].astype(F32) for i in range(3)]).astype(BF)


def backward_band(w_ref, j):
    return banded([jnp.transpose(w_ref[2 - i, j].astype(F32)) for i in range(3)]).astype(BF)


def pack_kernel(rows, feat_hbm, goal_hbm, w1_hbm, w2_hbm, even_ref, odd_ref, w1_ref, w2_ref, sems):
    odd = lax.rem(lax.axis_index("space"), 2)
    copies = []

    def start(source, target):
        copies.append(pltpu.make_async_copy(source, target, sems.at[len(copies)]))
        copies[-1].start()

    for which, ref in enumerate((even_ref, odd_ref)):
        bottom = jnp.where(odd == which, 1, 0)
        for source, count, at in ((feat_hbm, FEAT_HALO, 0), (goal_hbm, GOAL_HALO, FEAT_HALO)):
            start(source.at[pl.ds(bottom * (rows - count), count)], ref.at[at : at + count])
    start(w1_hbm, w1_ref)
    start(w2_hbm, w2_ref)
    for copy in copies:
        copy.wait()


def inner_kernel(
    rows,
    anchors_ref,
    w1_ref,
    w2_ref,
    b1_ref,
    b2_ref,
    feat,
    goal,
    back_hbm,
    first,
    hidden,
    deriv,
    misfit,
    slope,
    fwd1,
    fwd2,
    bwd2,
    bwd1_spread,
    biases,
    col_wave_ref,
    acc1,
    acc2,
    sum1,
    sum2,
    bwd1,
    back,
    sem,
):
    ch, cols = feat.shape[1:]
    half, pair = ch // 2, 2 * ch
    me = lax.axis_index("space")
    do = Stage(ch, cols)
    for j in range(3):
        spot = slice(pair * j, pair * (j + 1))
        fwd1[spot] = forward_band(w1_ref, j)
        fwd2[spot] = forward_band(w2_ref, j)
        band = backward_band(w1_ref, j)
        bwd1_spread[spot] = band
        bwd1[:, 4 * ch * j : 4 * ch * (j + 1)] = band
        bwd2[:, 4 * ch * j : 4 * ch * (j + 1)] = backward_band(w2_ref, j)
    biases[0] = bias_tile(b1_ref)
    biases[1] = bias_tile(b2_ref)
    row_wave = row_waves(anchors_ref, me * rows, half)
    col_wave_ref[...] = col_waves(anchors_ref, half, cols)
    for total in (acc1, acc2, sum1, sum2):
        total[...] = jnp.zeros_like(total)
    for row in range(rows):
        first[do.rows(row, 1)] = with_geo(
            feat[row], row_wave[:, row : row + 1], col_wave_ref[...]
        ).astype(BF)
    F, H, D = view((first, 0, rows)), view((hidden, 0, rows - 2)), view((deriv, 0, rows - 2))
    M, S = view((misfit, 0, rows - 4)), view((slope, 0, rows - 6))

    def conv_one(r):
        do.forward_one(fwd1, biases[0], F, r - 1, hidden, r - 1, deriv, r - 1)

    def conv_two(r):
        goals = jnp.concatenate([goal[r], goal[r + 1]], axis=0)
        do.forward_two(fwd2, biases[1], H, r - 2, goals, misfit, r - 2, sum2)

    def grad_two(r):
        do.weight_grad(acc2, M, r - 2, H, r - 2)

    def bend(r):
        do.backward_two(bwd2, M, r - 3, D, r - 1, slope, r - 3, sum1)

    def grad_one(r):
        do.weight_grad(acc1, S, r - 3, F, r - 1)

    def input_grad(r):
        value = do.back(bwd1, S, r - 4).astype(BF)
        back[r - 4] = value[:ch]
        back[r - 3] = value[ch:]

    steps = (
        (grad_one, 4, rows - 6, 6),
        (input_grad, 4, rows - 6, 6),
        (bend, 3, rows - 5, 4),
        (grad_two, 2, rows - 4, 3),
        (conv_two, 2, rows - 4, 2),
        (conv_one, 1, rows - 3, 0),
    )
    for turn in range(rows // 2 + 3):
        for step, low, high, lag in steps:
            r = low + 2 * (turn - lag)
            if low <= r <= high:
                step(r)
    copy = pltpu.make_async_copy(back, back_hbm.at[4 : rows - 4], sem)
    copy.start()
    copy.wait()


def edge_kernel(
    rows,
    size,
    factor,
    anchors_ref,
    fwd1,
    fwd2,
    bwd2,
    biases,
    col_wave_ref,
    old1,
    old2,
    old_sum1,
    old_sum2,
    goal,
    even_halo,
    odd_halo,
    first,
    hidden,
    deriv,
    misfit,
    slope,
    grads_ref,
    slope_out,
    new_first,
    new_hidden,
    new_deriv,
    new_misfit,
    new_slope,
    acc1,
    acc2,
    sum1,
    sum2,
):
    ch, cols = goal.shape[1:]
    half = ch // 2
    me = lax.axis_index("space")
    above = (me > 0).astype(jnp.int32)
    below = (me < size - 1).astype(jnp.int32)
    odd = lax.rem(me, 2)
    do = Stage(ch, cols)
    flags = (above, below)

    def halo(side, k):
        return jnp.where(odd == side, odd_halo[k], even_halo[k])

    acc1[...] = old1[...]
    acc2[...] = old2[...]
    sum1[...] = old_sum1[...]
    sum2[...] = old_sum2[...]
    for side, start in enumerate((-4, rows)):
        row_wave = row_waves(anchors_ref, me * rows + start, half)
        for k in range(4):
            value = with_geo(halo(side, k), row_wave[:, k : k + 1], col_wave_ref[...])
            new_first[side, do.rows(k, 1)] = keep(flags[side], value).astype(BF)
    top, low = 0, 1
    nF, nH, nD, nM, nS = (
        [ref.at[0], ref.at[1]] for ref in (new_first, new_hidden, new_deriv, new_misfit, new_slope)
    )
    F = (view((nF[top], 0, 4), (first, 0, 5)), view((first, rows - 5, 5), (nF[low], 0, 4)))
    H = (view((nH[top], 0, 4), (hidden, 0, 2)), view((hidden, rows - 4, 2), (nH[low], 0, 4)))
    D = (view((nD[top], 0, 2), (deriv, 0, 2)), view((deriv, rows - 4, 2), (nD[low], 0, 2)))
    M = (view((nM[top], 0, 4), (misfit, 0, 2)), view((misfit, rows - 6, 2), (nM[low], 0, 4)))
    S = (view((nS[top], 0, 4), (slope, 0, 2)), view((slope, rows - 8, 2), (nS[low], 0, 4)))
    one = functools.partial(do.forward_one, fwd1, biases[0])
    one(F[top], 2, nH[top], 2, nD[top], 0, low=above)
    one(F[low], 3, nH[low], 0, nD[low], 0, high=below)
    one(F[top], 0, nH[top], 0, low=above, high=above)
    one(F[low], 5, nH[low], 2, low=below, high=below)
    two = functools.partial(do.forward_two, fwd2, biases[1])
    two(H[top], 2, jnp.concatenate([goal[0], goal[1]], axis=0), nM[top], 2, sum2)
    two(
        H[low], 0, jnp.concatenate([goal[rows - 2], goal[rows - 1]], axis=0), nM[low], 0, sum2
    )
    two(H[top], 0, jnp.concatenate([halo(0, 4), halo(0, 5)], axis=0), nM[top], 0, sum2, above)
    two(H[low], 2, jnp.concatenate([halo(1, 4), halo(1, 5)], axis=0), nM[low], 2, sum2, below)
    bend = functools.partial(do.backward_two, bwd2)
    bend(M[top], 2, D[top], 2, nS[top], 2, sum1)
    bend(M[low], 0, D[low], 0, nS[low], 0, sum1)
    do.weight_grad(acc2, M[top], 2, H[top], 2)
    bend(M[top], 0, D[top], 0, nS[top], 0, sum1, low=above)
    bend(M[low], 2, D[low], 2, nS[low], 2, sum1, high=below)
    do.weight_grad(acc2, M[low], 2, H[low], 0)
    do.weight_grad(acc1, S[top], 3, F[top], 5)
    do.weight_grad(acc1, S[low], 1, F[low], 0)
    do.weight_grad(acc1, S[top], 1, F[top], 3)
    do.weight_grad(acc1, S[low], 3, F[low], 2)
    slope_out[...] = new_slope[:, 1]

    def emit(base, acc, total):
        summed = jnp.sum(total[...], axis=1, keepdims=True)
        side = jnp.broadcast_to(summed, (ch, ch))
        for j in range(3):
            upper = acc[2 * j * ch : (2 * j + 1) * ch]
            lower = acc[(2 * j + 1) * ch : (2 * j + 2) * ch]
            block = jnp.concatenate([upper[:, : 3 * ch] + lower[:, ch:], side], axis=1) * factor
            for t in range(ch // 8):
                for part in range(2):
                    grads_ref[base + (j * (ch // 8) + t) * 2 + part] = block[
                        8 * t : 8 * t + 8, 128 * part : 128 * part + 128
                    ]

    emit(0, acc1, sum1)
    emit(6 * (ch // 8), acc2, sum2)
    for spare in range(12 * (ch // 8), grads_ref.shape[0]):
        grads_ref[spare] = jnp.zeros((8, 128), F32)


def rest_kernel(rows, old_back, bwd1_spread, new_slope, slope, back_hbm, back, sems):
    ch = back.shape[2]
    do = Stage(ch, back.shape[3])
    inside = slope.at[1]
    S = (
        view((new_slope.at[0], 0, 4), (inside, 0, 2)),
        view((inside, rows - 8, 2), (new_slope.at[1], 0, 4)),
    )
    copies = []
    for side, r in enumerate((0, rows - 4)):
        for at in range(2):
            value = spread(bwd1_spread[...], S[side](2 * at, 4, ch), mirrored=True).astype(BF)
            back[side, 2 * at] = value[:ch]
            back[side, 2 * at + 1] = value[ch:]
        copy = pltpu.make_async_copy(back.at[side], back_hbm.at[r : r + 4], sems.at[side])
        copy.start()
        copies.append(copy)
    for copy in copies:
        copy.wait()


def sum_kernel(parts_ref, out_ref):
    total = jnp.sum(parts_ref[...], axis=0).astype(BF)
    out_ref[...] = jnp.broadcast_to(total[None], out_ref.shape)


def split_kernel(ch, full_ref, w1_ref, b1_ref, w2_ref, b2_ref):
    for base, w_ref, b_ref in ((0, w1_ref, b1_ref), (6 * (ch // 8), w2_ref, b2_ref)):
        for j in range(3):
            left, right = [
                jnp.concatenate(
                    [
                        full_ref[base + (j * (ch // 8) + t) * 2 + part].astype(F32)
                        for t in range(ch // 8)
                    ],
                    axis=0,
                )
                for part in range(2)
            ]
            w_ref[0, j] = left[:, :ch]
            w_ref[1, j] = left[:, ch:]
            w_ref[2, j] = right[:, :ch]
            if j == 0:
                b_ref[...] = jnp.transpose(right)[ch : ch + 1]


def shards(features, target, anchors, w_first, b_first, w_second, b_second):
    _, rows, ch, cols = features.shape
    size = lax.axis_size("space")
    devices = size * lax.axis_size("dp")
    factor = 1.0 / math.sqrt(features.shape[0] * devices * rows * cols)
    feats, goals = features[0], target[0]
    pair, quad = 2 * ch, 4 * ch

    links = [
        [
            link
            for low in range(first, size - 1, 2)
            for link in ((low, low + 1), (low + 1, low))
        ]
        for first in (0, 1)
    ]
    vmem = pl.BlockSpec(memory_space=pltpu.VMEM)
    smem = pl.BlockSpec(memory_space=pltpu.SMEM)
    hbm = pl.BlockSpec(memory_space=pltpu.HBM)

    def shape(*dims, dtype=BF):
        return jax.ShapeDtypeStruct(dims, dtype)

    def buffer(count, *lead, dtype=BF):
        return pltpu.VMEM(lead + (count * ch, cols), dtype)

    even_edge, odd_edge, w_first, w_second = pl.pallas_call(
        functools.partial(pack_kernel, rows),
        out_shape=(shape(FEAT_HALO + GOAL_HALO, ch, cols),) * 2 + (shape(3, 3, ch, ch),) * 2,
        in_specs=[hbm] * 4,
        out_specs=(vmem,) * 4,
        scratch_shapes=[pltpu.SemaphoreType.DMA((6,))],
        compiler_params=pltpu.CompilerParams(vmem_limit_bytes=8 << 20),
        name="pack",
    )(
        *(
            pltpu.with_memory_space_constraint(array, pltpu.HBM)
            for array in (feats, goals, w_first, w_second)
        )
    )
    odd_halo = lax.ppermute(odd_edge, "space", links[1])
    even_halo = lax.ppermute(even_edge, "space", links[0])
    (
        back,
        first,
        hidden,
        deriv,
        misfit,
        slope,
        fwd1,
        fwd2,
        bwd2,
        bwd1_spread,
        biases,
        col_wave,
        acc1,
        acc2,
        sum1,
        sum2,
    ) = pl.pallas_call(
        functools.partial(inner_kernel, rows),
        out_shape=(
            shape(rows, ch, cols),
            shape(rows * ch, cols),
            shape((rows - 2) * ch, cols),
            shape((rows - 2) * ch, cols, dtype=F32),
            shape(3, (rows - 4) * ch, cols),
            shape(3, (rows - 6) * ch, cols),
            shape(3 * pair, quad),
            shape(3 * pair, quad),
            shape(pair, 3 * quad),
            shape(3 * pair, quad),
            shape(2, pair, 128, dtype=F32),
            shape(ch // 2, cols, dtype=F32),
            shape(3 * pair, quad, dtype=F32),
            shape(3 * pair, quad, dtype=F32),
            shape(ch, 128, dtype=F32),
            shape(ch, 128, dtype=F32),
        ),
        in_specs=[smem] + [vmem] * 6,
        out_specs=(hbm,) + (vmem,) * 15,
        scratch_shapes=[
            pltpu.VMEM((pair, 3 * quad), BF),
            pltpu.VMEM((rows - 8, ch, cols), BF),
            pltpu.SemaphoreType.DMA,
        ],
        compiler_params=pltpu.CompilerParams(vmem_limit_bytes=24 << 20),
        cost_estimate=pl.CostEstimate(
            flops=14 * 10**9, bytes_accessed=12 * 10**6, transcendentals=10**6
        ),
        name="inner",
    )(
        anchors,
        w_first,
        w_second,
        b_first[None],
        b_second[None],
        feats,
        goals,
    )
    grads, new_slope = pl.pallas_call(
        functools.partial(edge_kernel, rows, size, factor),
        out_shape=(shape(devices, 8, 128, dtype=F32), shape(2, 4 * ch, cols)),
        in_specs=[smem] + [vmem] * 17,
        out_specs=(vmem,) * 2,
        scratch_shapes=[
            buffer(4, 2),
            buffer(4, 2),
            buffer(2, 2, dtype=F32),
            buffer(4, 2, 3),
            buffer(4, 2, 3),
            pltpu.VMEM((3 * pair, quad), F32),
            pltpu.VMEM((3 * pair, quad), F32),
            pltpu.VMEM((ch, 128), F32),
            pltpu.VMEM((ch, 128), F32),
        ],
        compiler_params=pltpu.CompilerParams(vmem_limit_bytes=24 << 20),
        cost_estimate=pl.CostEstimate(
            flops=9 * 10**9, bytes_accessed=10 * 10**6, transcendentals=5 * 10**5
        ),
        name="edges",
    )(
        anchors,
        fwd1,
        fwd2,
        bwd2,
        biases,
        col_wave,
        acc1,
        acc2,
        sum1,
        sum2,
        goals,
        even_halo,
        odd_halo,
        first,
        hidden,
        deriv,
        misfit,
        slope,
    )
    parts = lax.all_to_all(grads, AXES, 0, 0, tiled=True)
    back = pl.pallas_call(
        functools.partial(rest_kernel, rows),
        out_shape=shape(rows, ch, cols),
        in_specs=[hbm] + [vmem] * 3,
        out_specs=hbm,
        scratch_shapes=[
            pltpu.VMEM((2, 4, ch, cols), BF),
            pltpu.SemaphoreType.DMA((2,)),
        ],
        input_output_aliases={0: 0},
        compiler_params=pltpu.CompilerParams(vmem_limit_bytes=16 << 20),
        cost_estimate=pl.CostEstimate(
            flops=2 * 10**9, bytes_accessed=3 * 10**6, transcendentals=0
        ),
        name="rest",
    )(back, bwd1_spread, new_slope, slope)
    mine = pl.pallas_call(
        sum_kernel,
        out_shape=shape(devices, 8, 128),
        in_specs=[vmem],
        out_specs=vmem,
        compiler_params=pltpu.CompilerParams(vmem_limit_bytes=8 << 20),
        name="sum",
    )(parts)
    full = lax.all_to_all(mine, AXES, 0, 0, tiled=True)
    grad_w1, grad_b1, grad_w2, grad_b2 = pl.pallas_call(
        functools.partial(split_kernel, ch),
        out_shape=(
            shape(3, 3, ch, ch, dtype=F32),
            shape(1, ch, dtype=F32),
            shape(3, 3, ch, ch, dtype=F32),
            shape(1, ch, dtype=F32),
        ),
        in_specs=[vmem],
        out_specs=(vmem,) * 4,
        compiler_params=pltpu.CompilerParams(vmem_limit_bytes=8 << 20),
        name="split",
    )(full)
    return (back[None], grad_w1, grad_b1[0], grad_w2, grad_b2[0])


def solution(mesh):
    in_specs = (
        P("dp", "space", None, None),
        P("dp", "space", None, None),
        P("dp", None),
        P(),
        P(),
        P(),
        P(),
    )
    out_specs = (P("dp", "space", None, None), P(), P(), P(), P())
    return jax.shard_map(
        shards, mesh=mesh, in_specs=in_specs, out_specs=out_specs, check_vma=False
    )
```

time: 80.9 us -> 75.7 us (0.936)
  Pallas kernels: 30.6 us -> 25.5 us
  local copies, waits for them, and re-layouts: 3.98 us -> 2.13 us
  waiting for transfers between devices: 8.7 us -> 10.3 us
    pallas_call x1, Pallas kernels: 16.6 us -> 12.6 us  [shards(): pl.pallas_call(functools.partial(inner_kernel, rows), out_shape=(shape(ro...]
    ppermute x2, waiting for transfers between devices: 0.01 us -> 3.5 us  [the longest x1 3.5 us: shards(): even_halo = lax.ppermute(even_edge, 'space', links[0])]
    pallas_call x1, Pallas kernels: 9.78 us -> 7.25 us  [shards(): pl.pallas_call(functools.partial(edge_kernel, rows, size, factor), out_sh...]
    pallas_call x0 -> x2, Pallas kernels: none -> 2.5 us  [the longest x1 1.64 us: shards(): pl.pallas_call(functools.partial(pack_kernel, rows), out_shape=(shape(FEA...]
    dynamic_slice x2 -> x0, local copies, waits for them, and re-layouts: 2.49 us -> none  [the longest x1 1.42 us: edge(): lax.dynamic_slice_in_dim(feats, start, FEAT_HALO)]
    all_to_all x1, waiting for transfers between devices: 8.7 us -> 6.76 us  [shards(): full = lax.all_to_all(mine, AXES, 0, 0, tiled=True)]
    unnamed x16 -> x14, local copies, waits for them, and re-layouts: 0.75 us -> 2.13 us
    pallas_call x1, Pallas kernels: 1.88 us -> 0.93 us  [shards(): pl.pallas_call(functools.partial(split_kernel, ch), out_shape=(shape(3, 3...]
  transfers between devices with their start and end apart: 3 -> 3, of which waited for: 1 -> 2; matrix products, arithmetic and copies ran while one was open for 0% -> 0% of each run, Pallas kernels for 23% -> 20%
where the time goes in v3:
time: 75.7 us; the launch traced here: 75.4 us
  blocking collectives  29.4 us (39%)
  Pallas kernels  25.5 us (34%)
  waiting for transfers between devices  10.3 us (14%)
  starting transfers between devices  7.31 us (10%)
  local copies, waits for them, and re-layouts  2.13 us (3%)
  between operations  0.79 us (1%)
    all_to_all x1, blocking collectives, shards(): parts = lax.all_to_all(grads, AXES, 0, 0, tiled=True)  29.4 us
    pallas_call x1, Pallas kernels, shards(): pl.pallas_call(functools.partial(inner_kernel, rows), out_shape=(shape(ro...  12.6 us
    pallas_call x1, Pallas kernels, shards(): pl.pallas_call(functools.partial(edge_kernel, rows, size, factor), out_sh...  7.25 us
    all_to_all x1, waiting for transfers between devices, shards(): full = lax.all_to_all(mine, AXES, 0, 0, tiled=True)  6.76 us
    all_to_all x1, starting transfers between devices, shards(): full = lax.all_to_all(mine, AXES, 0, 0, tiled=True)  4.42 us
    ppermute x1, waiting for transfers between devices, shards(): even_halo = lax.ppermute(even_edge, 'space', links[0])  3.5 us
    pallas_call x1, Pallas kernels, shards(): pl.pallas_call(functools.partial(rest_kernel, rows), out_shape=shape(rows...  2.21 us
    ppermute x1, starting transfers between devices, shards(): even_halo = lax.ppermute(even_edge, 'space', links[0])  2.19 us
  transfers between devices with their start and end apart: 3, of which 2 were waited for; matrix products, arithmetic and copies ran while one was open for 0% of the time, Pallas kernels for 20%

profile of v3, /device:TPU:1, one launch (start us, length us, event | category | flops | bytes accessed | tf_op | source)
XLA Modules:
  0.0 75.4 jit_solution(2560607694558123680)
XLA Ops:
  0.6 0.0 copy-start.2
  0.6 0.0 copy-start.3
  0.7 0.0 copy-start.4
  0.7 0.0 copy-start.5
  0.7 0.0 copy-start.6
  0.7 1.6 %pack.1 = (bf16[6,64,1024]{2,1,0:T(8,128)(2,1)S(1)}, bf16[6,64,1024]{2,1,0:T(8,128)(2,1)S(1)}, bf16[3,3,64,64]{3,2,1,0:T(8,128)(2,1)S(1)}, bf16[3,3,64,64]{3,2,1,0:T(8,128)(2,1)S(1)}) custom-call(bf16[16,64,1024]{2,1,0:T(8,128)(2,1)} %bitcast.7, bf16[16,64,1024]{2,1,0:T(8,128)(2,1)} %bitcast.9, bf16[3,3,64,64]{3,2,1,0:T(8,128)(2,1)} %w1_hbm.1, ...), custom_call_target="tpu_custom_call" | custom-call | tf_op jit(solution)/shard_map/pack/pallas_call | solution.py:489
  2.3 2.2 %collective-permute-start = (bf16[6,64,1024]{2,1,0:T(8,128)(2,1)S(1)}, bf16[6,64,1024]{2,1,0:T(8,128)(2,1)S(1)}, u32[]{:S(2)}, u32[]{:S(2)}) collective-permute-start(bf16[6,64,1024]{2,1,0:T(8,128)(2,1)S(1)} %get-tuple-element.44), channel_id=1, source_target_pairs={{0,1},{1,0},{2,3},{3,2},{4,5},{5,4},{6,7},{7,6},{8,9},{9,8},{10,11... | collective-permute-start | bytes 2359304 | tf_op jit(solution)/shard_map/ppermute | solution.py:504
  4.5 0.7 collective-permute-start.1
  5.2 0.0 copy-done.2
  5.2 0.0 copy-done.3
  5.3 0.0 copy-done.4
  5.3 0.0 copy-done.5
  5.3 0.0 copy-done.6
  5.3 12.6 %inner.1 = (bf16[16,64,1024]{2,1,0:T(8,128)(2,1)}, bf16[1024,1024]{1,0:T(8,128)(2,1)S(1)}, bf16[896,1024]{1,0:T(8,128)(2,1)S(1)}, f32[896,1024]{1,0:T(8,128)S(1)...) custom-call(s32[1,2]{1,0:T(1,128)S(1)} %copy-done.6, ...), custom_call_target="tpu_custom_call" | custom-call | flops 14000000000 | bytes 12000000 | tf_op jit(solution)/shard_map/inner/pallas_call | solution.py:522
  17.9 0.0 copy-start
  17.9 3.5 %collective-permute-done.even_halo = bf16[6,64,1024]{2,1,0:T(8,128)(2,1)S(1)} collective-permute-done((bf16[6,64,1024]{2,1,0:T(8,128)(2,1)S(1)}, bf16[6,64,1024]{2,1,0:T(8,128)(2,1)S(1)}, u32[]{:S(2)}, u32[]{:S(2)}) %collective-permute-start) | collective-permute-done | bytes 786464 | tf_op jit(solution)/shard_map/ppermute | solution.py:504
  21.4 0.0 collective-permute-done.1.odd_halo
  21.4 7.2 %edges.1 = (f32[128,8,128]{2,1,0:T(8,128)S(1)}, bf16[2,256,1024]{2,1,0:T(8,128)(2,1)S(1)}) custom-call(s32[1,2]{1,0:T(1,128)S(1)} %copy-done.6, bf16[384,256]{1,0:T(8,128)(2,1)S(1)} %get-tuple-element.35.fwd1, bf16[384,256]{1,0:T(8,128)(2,1)S(1)} %get-tuple-element.36.fwd2, bf16[128,768]{1,0:T(8,128)(2,1)S(1)} %get-tuple-element.37.bwd2, ...), custom_call_target="tpu_custom_call" | custom-call | flops 8999999488 | bytes 10000000 | tf_op jit(solution)/shard_map/edges/pallas_call | solution.py:563
  28.7 0.0 copy-done
  28.7 29.4 %all_to_all.10.parts_ref = f32[128,8,128]{2,1,0:T(8,128)S(1)} all-to-all(f32[128,8,128]{2,1,0:T(8,128)S(1)} %get-tuple-element.52), channel_id=1, replica_groups=mesh['dp'=16,'space'=8] {'dp','space'}, dimensions={0} | all-to-all | bytes 1048576 | tf_op jit(solution)/shard_map/all_to_all | solution.py:604
  58.2 0.9 %sum.1 = bf16[128,8,128]{2,1,0:T(8,128)(2,1)} custom-call(f32[128,8,128]{2,1,0:T(8,128)S(1)} %all_to_all.10.parts_ref), custom_call_target="tpu_custom_call" | custom-call | tf_op jit(solution)/shard_map/sum/pallas_call | solution.py:621
  59.0 4.4 %all-to-all-start.1 = ((bf16[128,8,128]{2,1,0:T(8,128)(2,1)}), bf16[128,8,128]{2,1,0:T(8,128)(2,1)S(1)}, u32[]{:S(2)}, u32[]{:S(2)}) async-start(bf16[128,8,128]{2,1,0:T(8,128)(2,1)} %sum.1), calls=%async_computation.1 | async-start | bytes 524288 | tf_op jit(solution)/shard_map/all_to_all | solution.py:629
  63.4 0.0 copy-start.1
  63.4 2.1 %copy-done.1 = bf16[3,640,1024]{2,1,0:T(8,128)(2,1)S(1)} copy-done((bf16[3,640,1024]{2,1,0:T(8,128)(2,1)S(1)}, bf16[3,640,1024]{2,1,0:T(8,128)(2,1)}, u32[]{:S(2)}) %copy-start.1) | copy-done | bytes 3932184
  65.5 2.2 %rest.1 = bf16[16,64,1024]{2,1,0:T(8,128)(2,1)} custom-call(bf16[16,64,1024]{2,1,0:T(8,128)(2,1)} %get-tuple-element.33.old_back, bf16[384,256]{1,0:T(8,128)(2,1)S(1)} %get-tuple-element.34.bwd1_spread, bf16[2,256,1024]{2,1,0:T(8,128)(2,1)S(1)} %get-tuple-element.51.new_slope, bf16[3,640,1024]{2,1,0:T(8,128)(2,1)S(1)} %copy-done.1), custom_call_target="tpu_custom_call", output_to_operand_aliasing={{}: (0, {})} | custom-call | flops 2000000000 | bytes 3000000 | tf_op jit(solution)/shard_map/rest/pallas_call | solution.py:605
  67.8 6.8 %all-to-all-done.1.full_ref = bf16[128,8,128]{2,1,0:T(8,128)(2,1)S(1)} async-done(((bf16[128,8,128]{2,1,0:T(8,128)(2,1)}), bf16[128,8,128]{2,1,0:T(8,128)(2,1)S(1)}, u32[]{:S(2)}, u32[]{:S(2)}) %all-to-all-start.1) | async-done | bytes 262176 | tf_op jit(solution)/shard_map/all_to_all | solution.py:629
  74.5 0.9 %split.1 = (f32[3,3,64,64]{3,2,1,0:T(8,128)}, f32[1,64]{1,0:T(1,128)}, f32[3,3,64,64]{3,2,1,0:T(8,128)}, f32[1,64]{1,0:T(1,128)}) custom-call(bf16[128,8,128]{2,1,0:T(8,128)(2,1)S(1)} %all-to-all-done.1.full_ref), custom_call_target="tpu_custom_call" | custom-call | tf_op jit(solution)/shard_map/split/pallas_call | solution.py:630
Async XLA Ops:
  0.6 4.6 %copy-start.2 = (bf16[1,16,64,1024]{3,2,1,0:T(8,128)(2,1)S(1)}, bf16[1,16,64,1024]{3,2,1,0:T(8,128)(2,1)}, u32[]{:S(2)}) copy-start(bf16[1,16,64,1024]{3,2,1,0:T(8,128)(2,1)} %param.7) | copy-start | bytes 6291460
  0.6 4.6 %copy-start.3 = (bf16[1,16,64,1024]{3,2,1,0:T(8,128)(2,1)S(1)}, bf16[1,16,64,1024]{3,2,1,0:T(8,128)(2,1)}, u32[]{:S(2)}) copy-start(bf16[1,16,64,1024]{3,2,1,0:T(8,128)(2,1)} %param.8) | copy-start | bytes 6291460
  0.7 4.6 %copy-start.4 = (f32[64]{0:T(128)S(1)}, f32[64]{0:T(128)}, u32[]{:S(2)}) copy-start(f32[64]{0:T(128)} %param.11) | copy-start | bytes 772
  0.7 4.6 %copy-start.5 = (f32[64]{0:T(128)S(1)}, f32[64]{0:T(128)}, u32[]{:S(2)}) copy-start(f32[64]{0:T(128)} %param.13) | copy-start | bytes 772
  0.7 4.6 %copy-start.6 = (s32[1,2]{1,0:T(1,128)S(1)}, s32[1,2]{1,0:T(1,128)}, u32[]{:S(2)}) copy-start(s32[1,2]{1,0:T(1,128)} %anchors_ref.3) | copy-start | bytes 28
  2.3 19.1 %collective-permute-start = (bf16[6,64,1024]{2,1,0:T(8,128)(2,1)S(1)}, bf16[6,64,1024]{2,1,0:T(8,128)(2,1)S(1)}, u32[]{:S(2)}, u32[]{:S(2)}) collective-permute-start(bf16[6,64,1024]{2,1,0:T(8,128)(2,1)S(1)} %get-tuple-element.44), channel_id=1, source_target_pairs={{0,1},{1,0},{2,3},{3,2},{4,5},{5,4},{6,7},{7,6},{8,9},{9,8},{10,11... | collective-permute-start | bytes 2359304 | tf_op jit(solution)/shard_map/ppermute | solution.py:504
  4.5 16.9 %collective-permute-start.1 = (bf16[6,64,1024]{2,1,0:T(8,128)(2,1)S(1)}, bf16[6,64,1024]{2,1,0:T(8,128)(2,1)S(1)}, u32[]{:S(2)}, u32[]{:S(2)}) collective-permute-start(bf16[6,64,1024]{2,1,0:T(8,128)(2,1)S(1)} %get-tuple-element.45), channel_id=1, source_target_pairs={{1,2},{2,1},{3,4},{4,3},{5,6},{6,5},{9,10},{10,9},{11,12},{12,11},... | collective-permute-start | bytes 2359304 | tf_op jit(solution)/shard_map/ppermute | solution.py:503
  17.9 10.8 %copy-start = (bf16[3,640,1024]{2,1,0:T(8,128)(2,1)}, bf16[3,640,1024]{2,1,0:T(8,128)(2,1)S(1)}, u32[]{:S(2)}) copy-start(bf16[3,640,1024]{2,1,0:T(8,128)(2,1)S(1)} %get-tuple-element.50.slope) | copy-start | bytes 11796484
  59.0 15.5 %all-to-all-start.1 = ((bf16[128,8,128]{2,1,0:T(8,128)(2,1)}), bf16[128,8,128]{2,1,0:T(8,128)(2,1)S(1)}, u32[]{:S(2)}, u32[]{:S(2)}) async-start(bf16[128,8,128]{2,1,0:T(8,128)(2,1)} %sum.1), calls=%async_computation.1 | async-start | bytes 524288 | tf_op jit(solution)/shard_map/all_to_all | solution.py:629
  63.4 2.1 %copy-start.1 = (bf16[3,640,1024]{2,1,0:T(8,128)(2,1)S(1)}, bf16[3,640,1024]{2,1,0:T(8,128)(2,1)}, u32[]{:S(2)}) copy-start(bf16[3,640,1024]{2,1,0:T(8,128)(2,1)} %copy-done) | copy-start | bytes 11796484

commit v4 on v3

--- a/solution.py
+++ b/solution.py
@@ -11,8 +11,8 @@
 BF = jnp.bfloat16
 F32 = jnp.float32
 AXES = ("dp", "space")
-FEAT_HALO = 4
-GOAL_HALO = 2
+FEAT_HALO = 3
+GOAL_HALO = 1
 GELU_SCALE = math.sqrt(2.0 / math.pi)
 GELU_CUBE = 0.044715
 
@@ -330,6 +330,8 @@
     slope,
     grads_ref,
     slope_out,
+    even_send,
+    odd_send,
     new_first,
     new_hidden,
     new_deriv,
@@ -358,9 +360,11 @@
     sum2[...] = old_sum2[...]
     for side, start in enumerate((-4, rows)):
         row_wave = row_waves(anchors_ref, me * rows + start, half)
-        for k in range(4):
-            value = with_geo(halo(side, k), row_wave[:, k : k + 1], col_wave_ref[...])
-            new_first[side, do.rows(k, 1)] = keep(flags[side], value).astype(BF)
+        for k in range(FEAT_HALO):
+            lane = k + 1 - side
+            value = with_geo(halo(side, k), row_wave[:, lane : lane + 1], col_wave_ref[...])
+            new_first[side, do.rows(lane, 1)] = keep(flags[side], value).astype(BF)
+        new_first[side, do.rows(FEAT_HALO * side, 1)] = jnp.zeros((ch, cols), BF)
     top, low = 0, 1
     nF, nH, nD, nM, nS = (
         [ref.at[0], ref.at[1]] for ref in (new_first, new_hidden, new_deriv, new_misfit, new_slope)
@@ -376,12 +380,13 @@
     one(F[top], 0, nH[top], 0, low=above, high=above)
     one(F[low], 5, nH[low], 2, low=below, high=below)
     two = functools.partial(do.forward_two, fwd2, biases[1])
+    blank = jnp.zeros((ch, cols), BF)
     two(H[top], 2, jnp.concatenate([goal[0], goal[1]], axis=0), nM[top], 2, sum2)
     two(
         H[low], 0, jnp.concatenate([goal[rows - 2], goal[rows - 1]], axis=0), nM[low], 0, sum2
     )
-    two(H[top], 0, jnp.concatenate([halo(0, 4), halo(0, 5)], axis=0), nM[top], 0, sum2, above)
-    two(H[low], 2, jnp.concatenate([halo(1, 4), halo(1, 5)], axis=0), nM[low], 2, sum2, below)
+    two(H[top], 0, jnp.concatenate([blank, halo(0, FEAT_HALO)], axis=0), nM[top], 0, sum2, above)
+    two(H[low], 2, jnp.concatenate([halo(1, FEAT_HALO), blank], axis=0), nM[low], 2, sum2, below)
     bend = functools.partial(do.backward_two, bwd2)
     bend(M[top], 2, D[top], 2, nS[top], 2, sum1)
     bend(M[low], 0, D[low], 0, nS[low], 0, sum1)
@@ -394,6 +399,9 @@
     do.weight_grad(acc1, S[top], 1, F[top], 3)
     do.weight_grad(acc1, S[low], 3, F[low], 2)
     slope_out[...] = new_slope[:, 1]
+    highest, lowest = new_slope[top, 1, do.rows(1, 1)], new_slope[low, 1, do.rows(2, 1)]
+    even_send[...] = jnp.where(odd == 0, lowest, highest)
+    odd_send[...] = jnp.where(odd == 1, lowest, highest)
 
     def emit(base, acc, total):
         summed = jnp.sum(total[...], axis=1, keepdims=True)
@@ -406,26 +414,36 @@
                 for part in range(2):
                     grads_ref[base + (j * (ch // 8) + t) * 2 + part] = block[
                         8 * t : 8 * t + 8, 128 * part : 128 * part + 128
-                    ]
+                    ].astype(BF)
 
     emit(0, acc1, sum1)
     emit(6 * (ch // 8), acc2, sum2)
     for spare in range(12 * (ch // 8), grads_ref.shape[0]):
-        grads_ref[spare] = jnp.zeros((8, 128), F32)
-
-
-def rest_kernel(rows, old_back, bwd1_spread, new_slope, slope, back_hbm, back, sems):
+        grads_ref[spare] = jnp.zeros((8, 128), BF)
+
+
+def rest_kernel(
+    rows, old_back, bwd1_spread, new_slope, slope, even_slope, odd_slope, back_hbm, back, sems
+):
     ch = back.shape[2]
+    odd = lax.rem(lax.axis_index("space"), 2)
     do = Stage(ch, back.shape[3])
-    inside = slope.at[1]
-    S = (
-        view((new_slope.at[0], 0, 4), (inside, 0, 2)),
-        view((inside, rows - 8, 2), (new_slope.at[1], 0, 4)),
+    new, inside = [new_slope.at[0], new_slope.at[1]], slope.at[1]
+    outside = [jnp.where(odd == side, odd_slope[...], even_slope[...]) for side in range(2)]
+    blocks = (
+        (
+            jnp.concatenate([outside[0], new[0][do.rows(1, 3)]], axis=0),
+            jnp.concatenate([new[0][do.rows(2, 2)], inside[do.rows(0, 2)]], axis=0),
+        ),
+        (
+            jnp.concatenate([inside[do.rows(rows - 8, 2)], new[1][do.rows(0, 2)]], axis=0),
+            jnp.concatenate([new[1][do.rows(0, 3)], outside[1]], axis=0),
+        ),
     )
     copies = []
     for side, r in enumerate((0, rows - 4)):
         for at in range(2):
-            value = spread(bwd1_spread[...], S[side](2 * at, 4, ch), mirrored=True).astype(BF)
+            value = spread(bwd1_spread[...], blocks[side][at], mirrored=True).astype(BF)
             back[side, 2 * at] = value[:ch]
             back[side, 2 * at + 1] = value[ch:]
         copy = pltpu.make_async_copy(back.at[side], back_hbm.at[r : r + 4], sems.at[side])
@@ -436,7 +454,7 @@
 
 
 def sum_kernel(parts_ref, out_ref):
-    total = jnp.sum(parts_ref[...], axis=0).astype(BF)
+    total = jnp.sum(parts_ref[...].astype(F32), axis=0).astype(BF)
     out_ref[...] = jnp.broadcast_to(total[None], out_ref.shape)
 
 
@@ -560,11 +578,11 @@
         feats,
         goals,
     )
-    grads, new_slope = pl.pallas_call(
+    grads, new_slope, even_send, odd_send = pl.pallas_call(
         functools.partial(edge_kernel, rows, size, factor),
-        out_shape=(shape(devices, 8, 128, dtype=F32), shape(2, 4 * ch, cols)),
+        out_shape=(shape(devices, 8, 128), shape(2, 4 * ch, cols)) + (shape(ch, cols),) * 2,
         in_specs=[smem] + [vmem] * 17,
-        out_specs=(vmem,) * 2,
+        out_specs=(vmem,) * 4,
         scratch_shapes=[
             buffer(4, 2),
             buffer(4, 2),
@@ -602,10 +620,12 @@
         slope,
     )
     parts = lax.all_to_all(grads, AXES, 0, 0, tiled=True)
+    odd_slope = lax.ppermute(odd_send, "space", links[1])
+    even_slope = lax.ppermute(even_send, "space", links[0])
     back = pl.pallas_call(
         functools.partial(rest_kernel, rows),
         out_shape=shape(rows, ch, cols),
-        in_specs=[hbm] + [vmem] * 3,
+        in_specs=[hbm] + [vmem] * 5,
         out_specs=hbm,
         scratch_shapes=[
             pltpu.VMEM((2, 4, ch, cols), BF),
@@ -617,7 +637,7 @@
             flops=2 * 10**9, bytes_accessed=3 * 10**6, transcendentals=0
         ),
         name="rest",
-    )(back, bwd1_spread, new_slope, slope)
+    )(back, bwd1_spread, new_slope, slope, even_slope, odd_slope)
     mine = pl.pallas_call(
         sum_kernel,
         out_shape=shape(devices, 8, 128),

time: 75.7 us -> 68.1 us (0.90)
  blocking collectives: 29.4 us -> 0 us
  starting transfers between devices: 7.31 us -> 22.9 us
  waiting for transfers between devices: 10.3 us -> 15.7 us
  Pallas kernels: 25.5 us -> 26.3 us
    all_to_all x1 -> x0, blocking collectives: 29.4 us -> none  [shards(): parts = lax.all_to_all(grads, AXES, 0, 0, tiled=True)]
    all_to_all x0 -> x1, starting transfers between devices: none -> 13.6 us  [shards(): parts = lax.all_to_all(grads, AXES, 0, 0, tiled=True)]
    all_to_all x0 -> x1, waiting for transfers between devices: none -> 8.99 us  [shards(): parts = lax.all_to_all(grads, AXES, 0, 0, tiled=True)]
    ppermute x1, waiting for transfers between devices: 3.5 us -> 0.01 us  [shards(): even_halo = lax.ppermute(even_edge, 'space', links[0])]
    ppermute x0 -> x2, starting transfers between devices: none -> 2.09 us  [the longest x1 1.43 us: shards(): even_slope = lax.ppermute(even_send, 'space', links[0])]
  transfers between devices with their start and end apart: 3 -> 6, of which waited for: 2 -> 2; matrix products, arithmetic and copies ran while one was open for 0% -> 0% of each run, Pallas kernels for 20% -> 24%
where the time goes in v4:
time: 68.1 us; the launch traced here: 67.8 us
  Pallas kernels  26.3 us (39%)
  starting transfers between devices  22.9 us (34%)
  waiting for transfers between devices  15.7 us (23%)
  local copies, waits for them, and re-layouts  2.13 us (3%)
  between operations  0.82 us (1%)
    all_to_all x1, starting transfers between devices, shards(): parts = lax.all_to_all(grads, AXES, 0, 0, tiled=True)  13.6 us
    pallas_call x1, Pallas kernels, shards(): pl.pallas_call(functools.partial(inner_kernel, rows), out_shape=(shape(ro...  12.9 us
    all_to_all x1, waiting for transfers between devices, shards(): parts = lax.all_to_all(grads, AXES, 0, 0, tiled=True)  8.99 us
    pallas_call x1, Pallas kernels, shards(): pl.pallas_call(functools.partial(edge_kernel, rows, size, factor), out_sh...  7.85 us
    all_to_all x1, waiting for transfers between devices, shards(): full = lax.all_to_all(mine, AXES, 0, 0, tiled=True)  6.7 us
    all_to_all x1, starting transfers between devices, shards(): full = lax.all_to_all(mine, AXES, 0, 0, tiled=True)  4.35 us
    pallas_call x1, Pallas kernels, shards(): pl.pallas_call(functools.partial(rest_kernel, rows), out_shape=shape(rows...  2.24 us
    ppermute x1, starting transfers between devices, shards(): even_halo = lax.ppermute(even_edge, 'space', links[0])  2.19 us
  transfers between devices with their start and end apart: 6, of which 2 were waited for; matrix products, arithmetic and copies ran while one was open for 0% of the time, Pallas kernels for 24%

profile of v4, /device:TPU:1, one launch (start us, length us, event | category | flops | bytes accessed | tf_op | source)
XLA Modules:
  0.0 67.8 jit_solution(11738911727823978098)
XLA Ops:
  0.6 0.0 copy-start.2
  0.6 0.0 copy-start.3
  0.7 0.0 copy-start.4
  0.7 0.0 copy-start.5
  0.7 0.0 copy-start.6
  0.7 1.5 %pack.1 = (bf16[4,64,1024]{2,1,0:T(8,128)(2,1)S(1)}, bf16[4,64,1024]{2,1,0:T(8,128)(2,1)S(1)}, bf16[3,3,64,64]{3,2,1,0:T(8,128)(2,1)S(1)}, bf16[3,3,64,64]{3,2,1,0:T(8,128)(2,1)S(1)}) custom-call(bf16[16,64,1024]{2,1,0:T(8,128)(2,1)} %bitcast.7, bf16[16,64,1024]{2,1,0:T(8,128)(2,1)} %bitcast.9, bf16[3,3,64,64]{3,2,1,0:T(8,128)(2,1)} %w1_hbm.1, ...), custom_call_target="tpu_custom_call" | custom-call | tf_op jit(solution)/shard_map/pack/pallas_call | solution.py:507
  2.2 2.2 %collective-permute-start = (bf16[4,64,1024]{2,1,0:T(8,128)(2,1)S(1)}, bf16[4,64,1024]{2,1,0:T(8,128)(2,1)S(1)}, u32[]{:S(2)}, u32[]{:S(2)}) collective-permute-start(bf16[4,64,1024]{2,1,0:T(8,128)(2,1)S(1)} %get-tuple-element.46), channel_id=1, source_target_pairs={{0,1},{1,0},{2,3},{3,2},{4,5},{5,4},{6,7},{7,6},{8,9},{9,8},{10,11... | collective-permute-start | bytes 1572872 | tf_op jit(solution)/shard_map/ppermute | solution.py:522
  4.4 0.7 %collective-permute-start.1 = (bf16[4,64,1024]{2,1,0:T(8,128)(2,1)S(1)}, bf16[4,64,1024]{2,1,0:T(8,128)(2,1)S(1)}, u32[]{:S(2)}, u32[]{:S(2)}) collective-permute-start(bf16[4,64,1024]{2,1,0:T(8,128)(2,1)S(1)} %get-tuple-element.47), channel_id=1, source_target_pairs={{1,2},{2,1},{3,4},{4,3},{5,6},{6,5},{9,10},{10,9},{11,12},{12,11},... | collective-permute-start | bytes 1572872 | tf_op jit(solution)/shard_map/ppermute | solution.py:521
  5.1 0.0 copy-done.2
  5.1 0.0 copy-done.3
  5.1 0.0 copy-done.4
  5.1 0.0 copy-done.5
  5.1 0.0 copy-done.6
  5.1 12.9 %inner.1 = (bf16[16,64,1024]{2,1,0:T(8,128)(2,1)}, bf16[1024,1024]{1,0:T(8,128)(2,1)S(1)}, bf16[896,1024]{1,0:T(8,128)(2,1)S(1)}, f32[896,1024]{1,0:T(8,128)S(1)...) custom-call(s32[1,2]{1,0:T(1,128)S(1)} %copy-done.6, ...), custom_call_target="tpu_custom_call" | custom-call | flops 14000000000 | bytes 12000000 | tf_op jit(solution)/shard_map/inner/pallas_call | solution.py:540
  18.0 0.0 copy-start
  18.0 0.0 collective-permute-done.even_halo
  18.0 0.0 collective-permute-done.1.odd_halo
  18.0 7.8 %edges.1 = (bf16[128,8,128]{2,1,0:T(8,128)(2,1)}, bf16[2,256,1024]{2,1,0:T(8,128)(2,1)S(1)}, bf16[64,1024]{1,0:T(8,128)(2,1)S(1)}, bf16[64,1024]{1,0:T(8,128)(2,1)S(1)}) custom-call(s32[1,2]{1,0:T(1,128)S(1)} %copy-done.6, bf16[384,256]{1,0:T(8,128)(2,1)S(1)} %get-tuple-element.37.fwd1, bf16[384,256]{1,0:T(8,128)(2,1)S(1)} %get-tuple-element.38.fwd2, ...), custom_call_target="tpu_custom_call" | custom-call | flops 8999999488 | bytes 10000000 | tf_op jit(solution)/shard_map/edges/pallas_call | solution.py:581
  25.9 0.0 copy-done
  25.9 13.6 %all-to-all-start = ((bf16[128,8,128]{2,1,0:T(8,128)(2,1)}), bf16[128,8,128]{2,1,0:T(8,128)(2,1)S(1)}, u32[]{:S(2)}, u32[]{:S(2)}) async-start(bf16[128,8,128]{2,1,0:T(8,128)(2,1)} %get-tuple-element.56), calls=%async_computation | async-start | bytes 524288 | tf_op jit(solution)/shard_map/all_to_all | solution.py:622
  39.5 1.4 %collective-permute-start.2 = (bf16[64,1024]{1,0:T(8,128)(2,1)S(1)}, bf16[64,1024]{1,0:T(8,128)(2,1)S(1)}, u32[]{:S(2)}, u32[]{:S(2)}) collective-permute-start(bf16[64,1024]{1,0:T(8,128)(2,1)S(1)} %get-tuple-element.54), channel_id=1, source_target_pairs={{0,1},{1,0},{2,3},{3,2},{4,5},{5,4},{6,7},{7,6},{8,9},{9,8},{10,11... | collective-permute-start | bytes 393224 | tf_op jit(solution)/shard_map/ppermute | solution.py:624
  41.0 0.7 collective-permute-start.3
  41.6 9.0 %all-to-all-done.parts_ref = bf16[128,8,128]{2,1,0:T(8,128)(2,1)S(1)} async-done(((bf16[128,8,128]{2,1,0:T(8,128)(2,1)}), bf16[128,8,128]{2,1,0:T(8,128)(2,1)S(1)}, u32[]{:S(2)}, u32[]{:S(2)}) %all-to-all-start) | async-done | bytes 262176 | tf_op jit(solution)/shard_map/all_to_all | solution.py:622
  50.6 0.9 %sum.1 = bf16[128,8,128]{2,1,0:T(8,128)(2,1)} custom-call(bf16[128,8,128]{2,1,0:T(8,128)(2,1)S(1)} %all-to-all-done.parts_ref), custom_call_target="tpu_custom_call" | custom-call | tf_op jit(solution)/shard_map/sum/pallas_call | solution.py:641
  51.5 4.4 %all-to-all-start.1 = ((bf16[128,8,128]{2,1,0:T(8,128)(2,1)}), bf16[128,8,128]{2,1,0:T(8,128)(2,1)S(1)}, u32[]{:S(2)}, u32[]{:S(2)}) async-start(bf16[128,8,128]{2,1,0:T(8,128)(2,1)} %sum.1), calls=%async_computation.1 | async-start | bytes 524288 | tf_op jit(solution)/shard_map/all_to_all | solution.py:649
  55.8 0.0 collective-permute-done.2.even_slope
  55.8 0.0 collective-permute-done.3.odd_slope
  55.8 0.0 copy-start.1
  55.9 2.1 %copy-done.1 = bf16[3,640,1024]{2,1,0:T(8,128)(2,1)S(1)} copy-done((bf16[3,640,1024]{2,1,0:T(8,128)(2,1)S(1)}, bf16[3,640,1024]{2,1,0:T(8,128)(2,1)}, u32[]{:S(2)}) %copy-start.1) | copy-done | bytes 3932184
  58.0 2.2 %rest.1 = bf16[16,64,1024]{2,1,0:T(8,128)(2,1)} custom-call(bf16[16,64,1024]{2,1,0:T(8,128)(2,1)} %get-tuple-element.35.old_back, bf16[384,256]{1,0:T(8,128)(2,1)S(1)} %get-tuple-element.36.bwd1_spread, bf16[2,256,1024]{2,1,0:T(8,128)(2,1)S(1)} %get-tuple-element.53.new_slope, bf16[3,640,1024]{2,1,0:T(8,128)(2,1)S(1)} %copy-done.1, ...), custom_call_target="tpu_custom_call", output_to_operand_aliasing={{}: (0, {})} | custom-call | flops 2000000000 | bytes 3000000 | tf_op jit(solution)/shard_map/rest/pallas_call | solution.py:625
  60.2 6.7 %all-to-all-done.1.full_ref = bf16[128,8,128]{2,1,0:T(8,128)(2,1)S(1)} async-done(((bf16[128,8,128]{2,1,0:T(8,128)(2,1)}), bf16[128,8,128]{2,1,0:T(8,128)(2,1)S(1)}, u32[]{:S(2)}, u32[]{:S(2)}) %all-to-all-start.1) | async-done | bytes 262176 | tf_op jit(solution)/shard_map/all_to_all | solution.py:649
  66.9 0.9 %split.1 = (f32[3,3,64,64]{3,2,1,0:T(8,128)}, f32[1,64]{1,0:T(1,128)}, f32[3,3,64,64]{3,2,1,0:T(8,128)}, f32[1,64]{1,0:T(1,128)}) custom-call(bf16[128,8,128]{2,1,0:T(8,128)(2,1)S(1)} %all-to-all-done.1.full_ref), custom_call_target="tpu_custom_call" | custom-call | tf_op jit(solution)/shard_map/split/pallas_call | solution.py:650
Async XLA Ops:
  0.6 4.5 %copy-start.2 = (bf16[1,16,64,1024]{3,2,1,0:T(8,128)(2,1)S(1)}, bf16[1,16,64,1024]{3,2,1,0:T(8,128)(2,1)}, u32[]{:S(2)}) copy-start(bf16[1,16,64,1024]{3,2,1,0:T(8,128)(2,1)} %param.7) | copy-start | bytes 6291460
  0.6 4.5 %copy-start.3 = (bf16[1,16,64,1024]{3,2,1,0:T(8,128)(2,1)S(1)}, bf16[1,16,64,1024]{3,2,1,0:T(8,128)(2,1)}, u32[]{:S(2)}) copy-start(bf16[1,16,64,1024]{3,2,1,0:T(8,128)(2,1)} %param.8) | copy-start | bytes 6291460
  0.7 4.5 %copy-start.4 = (f32[64]{0:T(128)S(1)}, f32[64]{0:T(128)}, u32[]{:S(2)}) copy-start(f32[64]{0:T(128)} %param.11) | copy-start | bytes 772
  0.7 4.5 %copy-start.5 = (f32[64]{0:T(128)S(1)}, f32[64]{0:T(128)}, u32[]{:S(2)}) copy-start(f32[64]{0:T(128)} %param.13) | copy-start | bytes 772
  0.7 4.5 %copy-start.6 = (s32[1,2]{1,0:T(1,128)S(1)}, s32[1,2]{1,0:T(1,128)}, u32[]{:S(2)}) copy-start(s32[1,2]{1,0:T(1,128)} %anchors_ref.3) | copy-start | bytes 28
  2.2 15.8 %collective-permute-start = (bf16[4,64,1024]{2,1,0:T(8,128)(2,1)S(1)}, bf16[4,64,1024]{2,1,0:T(8,128)(2,1)S(1)}, u32[]{:S(2)}, u32[]{:S(2)}) collective-permute-start(bf16[4,64,1024]{2,1,0:T(8,128)(2,1)S(1)} %get-tuple-element.46), channel_id=1, source_target_pairs={{0,1},{1,0},{2,3},{3,2},{4,5},{5,4},{6,7},{7,6},{8,9},{9,8},{10,11... | collective-permute-start | bytes 1572872 | tf_op jit(solution)/shard_map/ppermute | solution.py:522
  4.4 13.6 %collective-permute-start.1 = (bf16[4,64,1024]{2,1,0:T(8,128)(2,1)S(1)}, bf16[4,64,1024]{2,1,0:T(8,128)(2,1)S(1)}, u32[]{:S(2)}, u32[]{:S(2)}) collective-permute-start(bf16[4,64,1024]{2,1,0:T(8,128)(2,1)S(1)} %get-tuple-element.47), channel_id=1, source_target_pairs={{1,2},{2,1},{3,4},{4,3},{5,6},{6,5},{9,10},{10,9},{11,12},{12,11},... | collective-permute-start | bytes 1572872 | tf_op jit(solution)/shard_map/ppermute | solution.py:521
  18.0 7.9 %copy-start = (bf16[3,640,1024]{2,1,0:T(8,128)(2,1)}, bf16[3,640,1024]{2,1,0:T(8,128)(2,1)S(1)}, u32[]{:S(2)}) copy-start(bf16[3,640,1024]{2,1,0:T(8,128)(2,1)S(1)} %get-tuple-element.52.slope) | copy-start | bytes 11796484
  25.9 24.7 %all-to-all-start = ((bf16[128,8,128]{2,1,0:T(8,128)(2,1)}), bf16[128,8,128]{2,1,0:T(8,128)(2,1)S(1)}, u32[]{:S(2)}, u32[]{:S(2)}) async-start(bf16[128,8,128]{2,1,0:T(8,128)(2,1)} %get-tuple-element.56), calls=%async_computation | async-start | bytes 524288 | tf_op jit(solution)/shard_map/all_to_all | solution.py:622
  39.5 16.3 %collective-permute-start.2 = (bf16[64,1024]{1,0:T(8,128)(2,1)S(1)}, bf16[64,1024]{1,0:T(8,128)(2,1)S(1)}, u32[]{:S(2)}, u32[]{:S(2)}) collective-permute-start(bf16[64,1024]{1,0:T(8,128)(2,1)S(1)} %get-tuple-element.54), channel_id=1, source_target_pairs={{0,1},{1,0},{2,3},{3,2},{4,5},{5,4},{6,7},{7,6},{8,9},{9,8},{10,11... | collective-permute-start | bytes 393224 | tf_op jit(solution)/shard_map/ppermute | solution.py:624
  41.0 14.9 %collective-permute-start.3 = (bf16[64,1024]{1,0:T(8,128)(2,1)S(1)}, bf16[64,1024]{1,0:T(8,128)(2,1)S(1)}, u32[]{:S(2)}, u32[]{:S(2)}) collective-permute-start(bf16[64,1024]{1,0:T(8,128)(2,1)S(1)} %get-tuple-element.55), channel_id=1, source_target_pairs={{1,2},{2,1},{3,4},{4,3},{5,6},{6,5},{9,10},{10,9},{11,12},{12,11},... | collective-permute-start | bytes 393224 | tf_op jit(solution)/shard_map/ppermute | solution.py:623
  51.5 15.4 %all-to-all-start.1 = ((bf16[128,8,128]{2,1,0:T(8,128)(2,1)}), bf16[128,8,128]{2,1,0:T(8,128)(2,1)S(1)}, u32[]{:S(2)}, u32[]{:S(2)}) async-start(bf16[128,8,128]{2,1,0:T(8,128)(2,1)} %sum.1), calls=%async_computation.1 | async-start | bytes 524288 | tf_op jit(solution)/shard_map/all_to_all | solution.py:649
  55.8 2.1 %copy-start.1 = (bf16[3,640,1024]{2,1,0:T(8,128)(2,1)S(1)}, bf16[3,640,1024]{2,1,0:T(8,128)(2,1)}, u32[]{:S(2)}) copy-start(bf16[3,640,1024]{2,1,0:T(8,128)(2,1)} %copy-done) | copy-start | bytes 11796484

commit v5 on v4

--- a/solution.py
+++ b/solution.py
@@ -130,7 +130,7 @@
         return jnp.tile(tile, (1, self.cols // 128))
 
     def put_three(self, target, at, value):
-        spot = self.rows(at, 2)
+        spot = self.rows(at, value.shape[0] // self.ch)
         target[0, spot] = to_left(value)
         target[1, spot] = value
         target[2, spot] = to_right(value)
@@ -151,6 +151,11 @@
         self.put_three(misfit, to, error)
         if flag is None:
             total[...] += lane_sum(error.astype(F32))
+
+    def one_row(self, matrix, bias, source, at, which):
+        ch = self.ch
+        bands = [matrix[(2 * j + which) * ch : (2 * j + which + 1) * ch] for j in range(3)]
+        return spread(jnp.concatenate(bands, axis=0), source(at, 4, ch)) + self.wide(bias[:ch])
 
     def three(self, source, at, count):
         return jnp.concatenate([source(at, count, self.ch, plane) for plane in range(3)], axis=0)
@@ -377,16 +382,22 @@
     one = functools.partial(do.forward_one, fwd1, biases[0])
     one(F[top], 2, nH[top], 2, nD[top], 0, low=above)
     one(F[low], 3, nH[low], 0, nD[low], 0, high=below)
-    one(F[top], 0, nH[top], 0, low=above, high=above)
-    one(F[low], 5, nH[low], 2, low=below, high=below)
+    blank = jnp.zeros((ch, cols), BF)
+    ends = ((top, 0, 1, 1, 0), (low, 5, 0, 2, 3))
+    for side, at, which, to, spare in ends:
+        value = activate(do.one_row(fwd1, biases[0], F[side], at, which))[0]
+        nH[side][do.rows(to, 1)] = keep(flags[side], value).astype(BF)
+        nH[side][do.rows(spare, 1)] = blank
     two = functools.partial(do.forward_two, fwd2, biases[1])
-    blank = jnp.zeros((ch, cols), BF)
     two(H[top], 2, jnp.concatenate([goal[0], goal[1]], axis=0), nM[top], 2, sum2)
     two(
         H[low], 0, jnp.concatenate([goal[rows - 2], goal[rows - 1]], axis=0), nM[low], 0, sum2
     )
-    two(H[top], 0, jnp.concatenate([blank, halo(0, FEAT_HALO)], axis=0), nM[top], 0, sum2, above)
-    two(H[low], 2, jnp.concatenate([halo(1, FEAT_HALO), blank], axis=0), nM[low], 2, sum2, below)
+    for side, at, which, to, spare in ((top, 0, 1, 1, 0), (low, 2, 0, 2, 3)):
+        out = do.one_row(fwd2, biases[1], H[side], at, which)
+        error = keep(flags[side], out - halo(side, FEAT_HALO).astype(F32))
+        do.put_three(nM[side], to, error.astype(BF))
+        do.put_three(nM[side], spare, blank)
     bend = functools.partial(do.backward_two, bwd2)
     bend(M[top], 2, D[top], 2, nS[top], 2, sum1)
     bend(M[low], 0, D[low], 0, nS[low], 0, sum1)

time: 68.1 us -> 67.4 us (0.990)
  Pallas kernels: 26.3 us -> 25.6 us
where the time goes in v5:
time: 67.4 us; the launch traced here: 67.2 us
  Pallas kernels  25.6 us (38%)
  starting transfers between devices  22.9 us (34%)
  waiting for transfers between devices  15.7 us (23%)
  local copies, waits for them, and re-layouts  2.13 us (3%)
  between operations  0.82 us (1%)
    all_to_all x1, starting transfers between devices, shards(): parts = lax.all_to_all(grads, AXES, 0, 0, tiled=True)  13.6 us
    pallas_call x1, Pallas kernels, shards(): pl.pallas_call(functools.partial(inner_kernel, rows), out_shape=(shape(ro...  12.9 us
    all_to_all x1, waiting for transfers between devices, shards(): parts = lax.all_to_all(grads, AXES, 0, 0, tiled=True)  8.99 us
    pallas_call x1, Pallas kernels, shards(): pl.pallas_call(functools.partial(edge_kernel, rows, size, factor), out_sh...  7.18 us
    all_to_all x1, waiting for transfers between devices, shards(): full = lax.all_to_all(mine, AXES, 0, 0, tiled=True)  6.69 us
    all_to_all x1, starting transfers between devices, shards(): full = lax.all_to_all(mine, AXES, 0, 0, tiled=True)  4.35 us
    pallas_call x1, Pallas kernels, shards(): pl.pallas_call(functools.partial(rest_kernel, rows), out_shape=shape(rows...  2.25 us
    ppermute x1, starting transfers between devices, shards(): even_halo = lax.ppermute(even_edge, 'space', links[0])  2.19 us
  transfers between devices with their start and end apart: 6, of which 2 were waited for; matrix products, arithmetic and copies ran while one was open for 0% of the time, Pallas kernels for 24%

profile of v5, /device:TPU:1, one launch (start us, length us, event | category | flops | bytes accessed | tf_op | source)
XLA Modules:
  0.0 67.2 jit_solution(13325776882816772006)
XLA Ops:
  0.6 0.0 copy-start.2
  0.6 0.0 copy-start.3
  0.7 0.0 copy-start.4
  0.7 0.0 copy-start.5
  0.7 0.0 copy-start.6
  0.7 1.5 %pack.1 = (bf16[4,64,1024]{2,1,0:T(8,128)(2,1)S(1)}, bf16[4,64,1024]{2,1,0:T(8,128)(2,1)S(1)}, bf16[3,3,64,64]{3,2,1,0:T(8,128)(2,1)S(1)}, bf16[3,3,64,64]{3,2,1,0:T(8,128)(2,1)S(1)}) custom-call(bf16[16,64,1024]{2,1,0:T(8,128)(2,1)} %bitcast.7, bf16[16,64,1024]{2,1,0:T(8,128)(2,1)} %bitcast.9, bf16[3,3,64,64]{3,2,1,0:T(8,128)(2,1)} %w1_hbm.1, ...), custom_call_target="tpu_custom_call" | custom-call | tf_op jit(solution)/shard_map/pack/pallas_call | solution.py:518
  2.2 2.2 %collective-permute-start = (bf16[4,64,1024]{2,1,0:T(8,128)(2,1)S(1)}, bf16[4,64,1024]{2,1,0:T(8,128)(2,1)S(1)}, u32[]{:S(2)}, u32[]{:S(2)}) collective-permute-start(bf16[4,64,1024]{2,1,0:T(8,128)(2,1)S(1)} %get-tuple-element.46), channel_id=1, source_target_pairs={{0,1},{1,0},{2,3},{3,2},{4,5},{5,4},{6,7},{7,6},{8,9},{9,8},{10,11... | collective-permute-start | bytes 1572872 | tf_op jit(solution)/shard_map/ppermute | solution.py:533
  4.4 0.7 %collective-permute-start.1 = (bf16[4,64,1024]{2,1,0:T(8,128)(2,1)S(1)}, bf16[4,64,1024]{2,1,0:T(8,128)(2,1)S(1)}, u32[]{:S(2)}, u32[]{:S(2)}) collective-permute-start(bf16[4,64,1024]{2,1,0:T(8,128)(2,1)S(1)} %get-tuple-element.47), channel_id=1, source_target_pairs={{1,2},{2,1},{3,4},{4,3},{5,6},{6,5},{9,10},{10,9},{11,12},{12,11},... | collective-permute-start | bytes 1572872 | tf_op jit(solution)/shard_map/ppermute | solution.py:532
  5.1 0.0 copy-done.2
  5.1 0.0 copy-done.3
  5.1 0.0 copy-done.4
  5.1 0.0 copy-done.5
  5.1 0.0 copy-done.6
  5.1 12.9 %inner.1 = (bf16[16,64,1024]{2,1,0:T(8,128)(2,1)}, bf16[1024,1024]{1,0:T(8,128)(2,1)S(1)}, bf16[896,1024]{1,0:T(8,128)(2,1)S(1)}, f32[896,1024]{1,0:T(8,128)S(1)...) custom-call(s32[1,2]{1,0:T(1,128)S(1)} %copy-done.6, ...), custom_call_target="tpu_custom_call" | custom-call | flops 14000000000 | bytes 12000000 | tf_op jit(solution)/shard_map/inner/pallas_call | solution.py:551
  18.0 0.0 copy-start
  18.0 0.0 collective-permute-done.even_halo
  18.0 0.0 collective-permute-done.1.odd_halo
  18.0 7.2 %edges.1 = (bf16[128,8,128]{2,1,0:T(8,128)(2,1)}, bf16[2,256,1024]{2,1,0:T(8,128)(2,1)S(1)}, bf16[64,1024]{1,0:T(8,128)(2,1)S(1)}, bf16[64,1024]{1,0:T(8,128)(2,1)S(1)}) custom-call(s32[1,2]{1,0:T(1,128)S(1)} %copy-done.6, bf16[384,256]{1,0:T(8,128)(2,1)S(1)} %get-tuple-element.37.fwd1, bf16[384,256]{1,0:T(8,128)(2,1)S(1)} %get-tuple-element.38.fwd2, ...), custom_call_target="tpu_custom_call" | custom-call | flops 8999999488 | bytes 10000000 | tf_op jit(solution)/shard_map/edges/pallas_call | solution.py:592
  25.2 0.0 copy-done
  25.2 13.6 %all-to-all-start = ((bf16[128,8,128]{2,1,0:T(8,128)(2,1)}), bf16[128,8,128]{2,1,0:T(8,128)(2,1)S(1)}, u32[]{:S(2)}, u32[]{:S(2)}) async-start(bf16[128,8,128]{2,1,0:T(8,128)(2,1)} %get-tuple-element.56), calls=%async_computation | async-start | bytes 524288 | tf_op jit(solution)/shard_map/all_to_all | solution.py:633
  38.8 1.4 %collective-permute-start.2 = (bf16[64,1024]{1,0:T(8,128)(2,1)S(1)}, bf16[64,1024]{1,0:T(8,128)(2,1)S(1)}, u32[]{:S(2)}, u32[]{:S(2)}) collective-permute-start(bf16[64,1024]{1,0:T(8,128)(2,1)S(1)} %get-tuple-element.54), channel_id=1, source_target_pairs={{0,1},{1,0},{2,3},{3,2},{4,5},{5,4},{6,7},{7,6},{8,9},{9,8},{10,11... | collective-permute-start | bytes 393224 | tf_op jit(solution)/shard_map/ppermute | solution.py:635
  40.3 0.7 collective-permute-start.3
  40.9 9.0 %all-to-all-done.parts_ref = bf16[128,8,128]{2,1,0:T(8,128)(2,1)S(1)} async-done(((bf16[128,8,128]{2,1,0:T(8,128)(2,1)}), bf16[128,8,128]{2,1,0:T(8,128)(2,1)S(1)}, u32[]{:S(2)}, u32[]{:S(2)}) %all-to-all-start) | async-done | bytes 262176 | tf_op jit(solution)/shard_map/all_to_all | solution.py:633
  49.9 0.9 %sum.1 = bf16[128,8,128]{2,1,0:T(8,128)(2,1)} custom-call(bf16[128,8,128]{2,1,0:T(8,128)(2,1)S(1)} %all-to-all-done.parts_ref), custom_call_target="tpu_custom_call" | custom-call | tf_op jit(solution)/shard_map/sum/pallas_call | solution.py:652
  50.8 4.4 %all-to-all-start.1 = ((bf16[128,8,128]{2,1,0:T(8,128)(2,1)}), bf16[128,8,128]{2,1,0:T(8,128)(2,1)S(1)}, u32[]{:S(2)}, u32[]{:S(2)}) async-start(bf16[128,8,128]{2,1,0:T(8,128)(2,1)} %sum.1), calls=%async_computation.1 | async-start | bytes 524288 | tf_op jit(solution)/shard_map/all_to_all | solution.py:660
  55.2 0.0 collective-permute-done.2.even_slope
  55.2 0.0 collective-permute-done.3.odd_slope
  55.2 0.0 copy-start.1
  55.2 2.1 %copy-done.1 = bf16[3,640,1024]{2,1,0:T(8,128)(2,1)S(1)} copy-done((bf16[3,640,1024]{2,1,0:T(8,128)(2,1)S(1)}, bf16[3,640,1024]{2,1,0:T(8,128)(2,1)}, u32[]{:S(2)}) %copy-start.1) | copy-done | bytes 3932184
  57.3 2.3 %rest.1 = bf16[16,64,1024]{2,1,0:T(8,128)(2,1)} custom-call(bf16[16,64,1024]{2,1,0:T(8,128)(2,1)} %get-tuple-element.35.old_back, bf16[384,256]{1,0:T(8,128)(2,1)S(1)} %get-tuple-element.36.bwd1_spread, bf16[2,256,1024]{2,1,0:T(8,128)(2,1)S(1)} %get-tuple-element.53.new_slope, bf16[3,640,1024]{2,1,0:T(8,128)(2,1)S(1)} %copy-done.1, ...), custom_call_target="tpu_custom_call", output_to_operand_aliasing={{}: (0, {})} | custom-call | flops 2000000000 | bytes 3000000 | tf_op jit(solution)/shard_map/rest/pallas_call | solution.py:636
  59.5 6.7 %all-to-all-done.1.full_ref = bf16[128,8,128]{2,1,0:T(8,128)(2,1)S(1)} async-done(((bf16[128,8,128]{2,1,0:T(8,128)(2,1)}), bf16[128,8,128]{2,1,0:T(8,128)(2,1)S(1)}, u32[]{:S(2)}, u32[]{:S(2)}) %all-to-all-start.1) | async-done | bytes 262176 | tf_op jit(solution)/shard_map/all_to_all | solution.py:660
  66.2 0.9 %split.1 = (f32[3,3,64,64]{3,2,1,0:T(8,128)}, f32[1,64]{1,0:T(1,128)}, f32[3,3,64,64]{3,2,1,0:T(8,128)}, f32[1,64]{1,0:T(1,128)}) custom-call(bf16[128,8,128]{2,1,0:T(8,128)(2,1)S(1)} %all-to-all-done.1.full_ref), custom_call_target="tpu_custom_call" | custom-call | tf_op jit(solution)/shard_map/split/pallas_call | solution.py:661
Async XLA Ops:
  0.6 4.5 %copy-start.2 = (bf16[1,16,64,1024]{3,2,1,0:T(8,128)(2,1)S(1)}, bf16[1,16,64,1024]{3,2,1,0:T(8,128)(2,1)}, u32[]{:S(2)}) copy-start(bf16[1,16,64,1024]{3,2,1,0:T(8,128)(2,1)} %param.7) | copy-start | bytes 6291460
  0.6 4.5 %copy-start.3 = (bf16[1,16,64,1024]{3,2,1,0:T(8,128)(2,1)S(1)}, bf16[1,16,64,1024]{3,2,1,0:T(8,128)(2,1)}, u32[]{:S(2)}) copy-start(bf16[1,16,64,1024]{3,2,1,0:T(8,128)(2,1)} %param.8) | copy-start | bytes 6291460
  0.7 4.5 %copy-start.4 = (f32[64]{0:T(128)S(1)}, f32[64]{0:T(128)}, u32[]{:S(2)}) copy-start(f32[64]{0:T(128)} %param.11) | copy-start | bytes 772
  0.7 4.5 %copy-start.5 = (f32[64]{0:T(128)S(1)}, f32[64]{0:T(128)}, u32[]{:S(2)}) copy-start(f32[64]{0:T(128)} %param.13) | copy-start | bytes 772
  0.7 4.5 %copy-start.6 = (s32[1,2]{1,0:T(1,128)S(1)}, s32[1,2]{1,0:T(1,128)}, u32[]{:S(2)}) copy-start(s32[1,2]{1,0:T(1,128)} %anchors_ref.3) | copy-start | bytes 28
  2.2 15.8 %collective-permute-start = (bf16[4,64,1024]{2,1,0:T(8,128)(2,1)S(1)}, bf16[4,64,1024]{2,1,0:T(8,128)(2,1)S(1)}, u32[]{:S(2)}, u32[]{:S(2)}) collective-permute-start(bf16[4,64,1024]{2,1,0:T(8,128)(2,1)S(1)} %get-tuple-element.46), channel_id=1, source_target_pairs={{0,1},{1,0},{2,3},{3,2},{4,5},{5,4},{6,7},{7,6},{8,9},{9,8},{10,11... | collective-permute-start | bytes 1572872 | tf_op jit(solution)/shard_map/ppermute | solution.py:533
  4.4 13.6 %collective-permute-start.1 = (bf16[4,64,1024]{2,1,0:T(8,128)(2,1)S(1)}, bf16[4,64,1024]{2,1,0:T(8,128)(2,1)S(1)}, u32[]{:S(2)}, u32[]{:S(2)}) collective-permute-start(bf16[4,64,1024]{2,1,0:T(8,128)(2,1)S(1)} %get-tuple-element.47), channel_id=1, source_target_pairs={{1,2},{2,1},{3,4},{4,3},{5,6},{6,5},{9,10},{10,9},{11,12},{12,11},... | collective-permute-start | bytes 1572872 | tf_op jit(solution)/shard_map/ppermute | solution.py:532
  18.0 7.2 %copy-start = (bf16[3,640,1024]{2,1,0:T(8,128)(2,1)}, bf16[3,640,1024]{2,1,0:T(8,128)(2,1)S(1)}, u32[]{:S(2)}) copy-start(bf16[3,640,1024]{2,1,0:T(8,128)(2,1)S(1)} %get-tuple-element.52.slope) | copy-start | bytes 11796484
  25.2 24.7 %all-to-all-start = ((bf16[128,8,128]{2,1,0:T(8,128)(2,1)}), bf16[128,8,128]{2,1,0:T(8,128)(2,1)S(1)}, u32[]{:S(2)}, u32[]{:S(2)}) async-start(bf16[128,8,128]{2,1,0:T(8,128)(2,1)} %get-tuple-element.56), calls=%async_computation | async-start | bytes 524288 | tf_op jit(solution)/shard_map/all_to_all | solution.py:633
  38.8 16.3 %collective-permute-start.2 = (bf16[64,1024]{1,0:T(8,128)(2,1)S(1)}, bf16[64,1024]{1,0:T(8,128)(2,1)S(1)}, u32[]{:S(2)}, u32[]{:S(2)}) collective-permute-start(bf16[64,1024]{1,0:T(8,128)(2,1)S(1)} %get-tuple-element.54), channel_id=1, source_target_pairs={{0,1},{1,0},{2,3},{3,2},{4,5},{5,4},{6,7},{7,6},{8,9},{9,8},{10,11... | collective-permute-start | bytes 393224 | tf_op jit(solution)/shard_map/ppermute | solution.py:635
  40.3 14.9 %collective-permute-start.3 = (bf16[64,1024]{1,0:T(8,128)(2,1)S(1)}, bf16[64,1024]{1,0:T(8,128)(2,1)S(1)}, u32[]{:S(2)}, u32[]{:S(2)}) collective-permute-start(bf16[64,1024]{1,0:T(8,128)(2,1)S(1)} %get-tuple-element.55), channel_id=1, source_target_pairs={{1,2},{2,1},{3,4},{4,3},{5,6},{6,5},{9,10},{10,9},{11,12},{12,11},... | collective-permute-start | bytes 393224 | tf_op jit(solution)/shard_map/ppermute | solution.py:634
  50.8 15.4 %all-to-all-start.1 = ((bf16[128,8,128]{2,1,0:T(8,128)(2,1)}), bf16[128,8,128]{2,1,0:T(8,128)(2,1)S(1)}, u32[]{:S(2)}, u32[]{:S(2)}) async-start(bf16[128,8,128]{2,1,0:T(8,128)(2,1)} %sum.1), calls=%async_computation.1 | async-start | bytes 524288 | tf_op jit(solution)/shard_map/all_to_all | solution.py:660
  55.2 2.1 %copy-start.1 = (bf16[3,640,1024]{2,1,0:T(8,128)(2,1)S(1)}, bf16[3,640,1024]{2,1,0:T(8,128)(2,1)}, u32[]{:S(2)}) copy-start(bf16[3,640,1024]{2,1,0:T(8,128)(2,1)} %copy-done) | copy-start | bytes 11796484
